TPU v7x, 32 devices: a whole 2x2x4 slice. The times are simulated.
32 devices in a mesh: section: 4 (over y, x), space: 8 (over z, core).
Axes of the slice: x: 2, y: 2, z: 4, core: 2. Of those that a mesh axis runs over, the one named last changes fastest.
Arguments:
- start_state: float32 [8, 6, 64, 512], P(None, None, 'space'), may hold values from -6 to 6
- stiffness: float32 [2, 64, 512], P(None, 'space'), may hold values from 0.5 to 4
- contact_a: int32 [8, 8, 8], P('section', 'space'), may hold values from 0 to 31
- contact_b: int32 [8, 8, 8], P('section', 'space'), may hold values from 0 to 39
- pair_count: int32 [8, 8], P('section', 'space'), may hold values from 1 to 8, 36 in all within a row
- cotangent: float32 [8, 6, 64, 512], P(None, None, 'space'), may hold values from -6 to 6
Outputs:
- exit_state: float32 [4, 8, 6, 64, 512], P('section', None, None, 'space')
- incoming_state_gradient: float32 [4, 8, 6, 64, 512], P('section', None, None, 'space')
- stiffness_grad: float32 [2, 64, 512], P(None, 'space')
Inputs may be any that keep to these rules, and one draw needn't show every extreme that they name: Tiles are numbered within one device's band: contact_a over its own 8 rows, contact_b over those rows with one row added above and below, the upper added row first. Slots at or beyond pair_count are ignored; at every step some device has all 8 slots live.
All inputs are finite; a program needn't handle non-finite values.
Results may differ from a plain program's by a relative error of at most 0.0003.
Values sent between devices are 32-bit elements; how exact they have to be, the bound alone decides.
A program may use at most 64 MiB of HBM per device.

v0:
```python
import jax
import jax.numpy as jnp
from jax import lax
from jax.sharding import PartitionSpec as P

time_step = 0.1
damping = 0.98
rest_length = 1.0
contact_scale = 0.3
kernel_spread = 2.0
gravity = 0.5
tiny_length = 1e-06


def passed_along(value, axis, by):
    size = lax.axis_size(axis)
    pairs = [(i, i + by) for i in range(size) if 0 <= i + by < size]
    return lax.ppermute(value, axis, pairs)


def padded(value, sides, width):
    for axis, dim in sides:
        size, length = (lax.axis_size(axis), value.shape[dim])
        up = [(i, (i + 1) % size) for i in range(size - 1)]
        down = [(j, i) for i, j in up]
        last = lax.slice_in_dim(value, length - width, length, axis=dim)
        first = lax.slice_in_dim(value, 0, width, axis=dim)
        before = lax.ppermute(last, axis, up)
        after = lax.ppermute(first, axis, down)
        value = jnp.concatenate([before, value, after], axis=dim)
    return value


def spring(offset, edge_constant):
    length = jnp.sqrt(jnp.sum(offset * offset, axis=0) + tiny_length)
    return (edge_constant * (length - rest_length) / length)[None] * offset


def contact(points, extended, hits_a, hits_b, active):
    tiles_own = points.reshape(3, -1, 128)
    tiles_all = extended.reshape(3, -1, 128)
    own_points = jnp.einsum("pt,ctk->cpk", hits_a, tiles_own, precision=lax.Precision.HIGHEST)
    other_points = jnp.einsum("pt,ctk->cpk", hits_b, tiles_all, precision=lax.Precision.HIGHEST)
    separation = own_points[:, :, :, None] - other_points[:, :, None, :]
    spring_weights = (
        jnp.exp(-jnp.sum(separation * separation, axis=0) / kernel_spread) * active[:, None, None]
    )
    repulsion = (
        2.0 * contact_scale / kernel_spread * jnp.sum(spring_weights[None] * separation, axis=3)
    )
    placed = jnp.einsum("pt,cpk->ctk", hits_a, repulsion, precision=lax.Precision.HIGHEST)
    return placed.reshape(points.shape)


def local_step(extended, velocity, stiff_row, stiff_column, hits_a, hits_b, active):
    points = extended[:, 1:-1]
    row_width = points.shape[2]
    column_mask = (lax.broadcasted_iota(jnp.int32, (1, row_width), 1) < row_width - 1).astype(
        stiff_row.dtype
    )
    right_edge = stiff_row * column_mask
    left_edge = jnp.pad(right_edge[:, :-1], ((0, 0), (1, 0)))
    right_points = jnp.pad(points[:, :, 1:], ((0, 0), (0, 0), (0, 1)))
    left_points = jnp.pad(points[:, :, :-1], ((0, 0), (0, 0), (1, 0)))
    total_force = spring(right_points - points, right_edge) + spring(
        left_points - points, left_edge
    )
    total_force = total_force + spring(extended[:, :-2] - points, stiff_column[:-1])
    total_force = total_force + spring(extended[:, 2:] - points, stiff_column[1:])
    total_force = total_force + contact(points, extended, hits_a, hits_b, active)
    gravity_pull = jnp.zeros((3, 1, 1), total_force.dtype).at[2].set(-gravity)
    velocity_new = damping * (velocity + time_step * (total_force + gravity_pull))
    points_new = points + time_step * velocity_new
    return jnp.concatenate([points_new, velocity_new], axis=0)


def tables(first_tiles, second_tiles, live_count, tiles_own, tiles_all):
    slot_count = first_tiles.shape[0]
    hits_a = (
        first_tiles[:, None] == lax.broadcasted_iota(jnp.int32, (slot_count, tiles_own), 1)
    ).astype(jnp.float32)
    hits_b = (
        second_tiles[:, None] == lax.broadcasted_iota(jnp.int32, (slot_count, tiles_all), 1)
    ).astype(jnp.float32)
    active = (lax.iota(jnp.int32, slot_count) < live_count).astype(jnp.float32)
    return (hits_a, hits_b, active)


def on_device(start_state, stiffness, contact_a, contact_b, pair_count, cotangent):
    sections = lax.axis_size("section")
    section_index = lax.axis_index("section")
    space_index = lax.axis_index("space")
    micro_count, _, own_rows, row_width = start_state.shape
    steps_section = contact_a.shape[0]
    tiles_own = own_rows * row_width // 128
    tiles_all = (own_rows + 2) * row_width // 128
    total_rows = own_rows * lax.axis_size("space")
    global_rows = space_index * own_rows + lax.iota(jnp.int32, own_rows)
    row_mask = (global_rows < total_rows - 1).astype(jnp.float32)[:, None]
    stiff_row = stiffness[0]
    stiff_own = stiffness[1] * row_mask
    stiff_above = passed_along(stiff_own[-1:], "space", 1)
    stiff_column = jnp.concatenate([stiff_above, stiff_own], axis=0)
    batch_step = jax.vmap(local_step, in_axes=(0, 0, None, None, None, None, None))

    def extend(points):
        return padded(points, (("space", 2),), 1)

    def back_step(table, extended, velocity, adjoint):
        hits_a, hits_b, active = table

        def forward_one(extended_in, velocity_in, row_in, column_in):
            return batch_step(extended_in, velocity_in, row_in, column_in, hits_a, hits_b, active)

        _, pullback = jax.vjp(forward_one, extended, velocity, stiff_row, stiff_column)
        grad_extended, grad_velocity, part_row, part_column = pullback(adjoint)
        edge_rows = jnp.stack([grad_extended[:, :, 0], grad_extended[:, :, -1]], axis=2)
        neighbour = padded(edge_rows, (("space", 2),), 1)
        interior = grad_extended[:, :, 1:-1]
        interior = interior.at[:, :, 0].add(neighbour[:, :, 0]).at[:, :, -1].add(neighbour[:, :, 3])
        return (jnp.concatenate([interior, grad_velocity], axis=1), part_row, part_column)

    first_all, second_all, count_all = (
        lax.all_gather(contact_a, "section", axis=0, tiled=True),
        lax.all_gather(contact_b, "section", axis=0, tiled=True),
        lax.all_gather(pair_count, "section", axis=0, tiled=True),
    )
    share = micro_count // sections
    own_start = lax.dynamic_slice_in_dim(start_state, section_index * share, share, 0)
    own_cotangent = lax.dynamic_slice_in_dim(cotangent, section_index * share, share, 0)
    numbers = jnp.arange(steps_section * sections, dtype=jnp.int32)

    def table_at(section_total):
        return tables(
            first_all[section_total, 0],
            second_all[section_total, 0],
            count_all[section_total, 0],
            tiles_own,
            tiles_all,
        )

    def forward_step(state_now, section_total):
        extended = extend(state_now[:, :3])
        hits_a, hits_b, active = table_at(section_total)
        moved = batch_step(
            extended, state_now[:, 3:], stiff_row, stiff_column, hits_a, hits_b, active
        )
        return (moved, (moved, extended, state_now[:, 3:]))

    _, (after_all, extended_all, velocity_all) = lax.scan(forward_step, own_start, numbers)

    def backward_step(carried, inputs):
        adjoint, grad_row, grad_column = carried
        section_total, extended, velocity = inputs
        adjoint, part_row, part_column = back_step(
            table_at(section_total), extended, velocity, adjoint
        )
        return ((adjoint, grad_row + part_row, grad_column + part_column), adjoint)

    start_carry = (own_cotangent, jnp.zeros_like(stiff_row), jnp.zeros_like(stiff_column))
    (_, grad_row, grad_column), before_all = lax.scan(
        backward_step, start_carry, (numbers, extended_all, velocity_all), reverse=True
    )
    exit_local = after_all[steps_section - 1 :: steps_section]
    adjoint_local = before_all[::steps_section]
    exit_result, resulting_adjoint = (
        lax.all_to_all(exit_local, "section", split_axis=0, concat_axis=1, tiled=True),
        lax.all_to_all(adjoint_local, "section", split_axis=0, concat_axis=1, tiled=True),
    )
    upper_part = passed_along(grad_column[:1], "space", -1)
    column_own = grad_column[1:].at[-1].add(upper_part[0]) * row_mask
    summed_row, summed_column = lax.psum((grad_row, column_own), "section")
    return (exit_result, resulting_adjoint, jnp.stack([summed_row, summed_column]))


def solution(mesh):
    in_specs = (
        P(None, None, "space", None),
        P(None, "space", None),
        P("section", "space", None),
        P("section", "space", None),
        P("section", "space"),
        P(None, None, "space", None),
    )
    out_specs = (
        P("section", None, None, "space", None),
        P("section", None, None, "space", None),
        P(None, "space", None),
    )
    return jax.shard_map(
        on_device, mesh=mesh, in_specs=in_specs, out_specs=out_specs, check_vma=False
    )
```

profile of v0, /device:TPU:0, one launch (start us, length us, event | category | flops | bytes accessed | tf_op | source)
XLA Modules:
  0.0 356.8 jit_solution(7042950477782283868)
XLA Ops:
  1.5 2.4 collective-permute-start.4
  8.3 8.2 %all-reduce.14 = s32[8]{0:T(128)S(1)} all-reduce(s32[8]{0:T(128)S(1)} %bitcast_dynamic-update-slice_fusion.3), channel_id=1, replica_groups=mesh['section'=4,'space'=8] {'section'}, use_global_device_ids=true, to_apply=%add.14 | all-reduce | flops 8 | bytes 64
  16.5 8.1 %all_gather.9 = s32[8,1,8]{2,1,0:T(1,128)S(1)} all-gather(s32[2,1,8]{2,1,0:T(1,128)} %param.20), channel_id=1, replica_groups=mesh['section'=4,'space'=8] {'section'}, dimensions={0}, use_global_device_ids=true | all-gather | bytes 320 | tf_op jit(solution)/shard_map/all_gather | solution.py:124
  24.6 7.2 %all_gather.10 = s32[8,1,8]{2,1,0:T(1,128)S(1)} all-gather(s32[2,1,8]{2,1,0:T(1,128)} %param.21), channel_id=1, replica_groups=mesh['section'=4,'space'=8] {'section'}, dimensions={0}, use_global_device_ids=true | all-gather | bytes 320 | tf_op jit(solution)/shard_map/all_gather | solution.py:125
  32.0 116.7 %while.43 = (s32[]{:T(128)}, f32[2,6,8,512]{3,2,1,0:T(8,128)S(1)}, f32[8,2,6,8,512]{4,3,2,1,0:T(8,128)S(1)}, f32[8,2,3,10,512]{4,3,2,1,0:T(8,128)}, f32[8,512]{1...) while((s32[]{:T(128)}, f32[2,6,8,512]{3,2,1,0:T(8,128)S(1)}, ...), condition=%wide.region_7.8_spmd, body=%wide.region_0.7_spmd.sunk | while | flops 14022485 | bytes 9260103 | solution.py:150
  33.4 3.0 collective-permute-start.1
  42.3 1.9 fusion.97
  46.9 3.9 %collective-permute-start.1 = (f32[2,3,1,512]{3,2,1,0:T(1,128)S(1)}, f32[2,3,1,512]{3,2,1,0:T(1,128)S(1)}, u32[]{:S(2)}, u32[]{:S(2)}) collective-permute-start(f32[2,3,1,512]{3,2,1,0:T(1,128)S(1)} %get-tuple-element.906), channel_id=1, source_target_pairs={{0,1},{1,2},{2,3},{3,4},{4,5},{5,6},{6,7},{8,9},{9,10},{10,11},{11... | collective-permute-start | bytes 36872 | tf_op jit(solution)/shard_map/while/body/eval_jaxpr/ppermute | solution.py:28
  56.7 1.9 fusion.97
  61.3 4.3 %collective-permute-start.1 = (f32[2,3,1,512]{3,2,1,0:T(1,128)S(1)}, f32[2,3,1,512]{3,2,1,0:T(1,128)S(1)}, u32[]{:S(2)}, u32[]{:S(2)}) collective-permute-start(f32[2,3,1,512]{3,2,1,0:T(1,128)S(1)} %get-tuple-element.906), channel_id=1, source_target_pairs={{0,1},{1,2},{2,3},{3,4},{4,5},{5,6},{6,7},{8,9},{9,10},{10,11},{11... | collective-permute-start | bytes 36872 | tf_op jit(solution)/shard_map/while/body/eval_jaxpr/ppermute | solution.py:28
  71.5 1.9 fusion.97
  76.1 4.3 %collective-permute-start.1 = (f32[2,3,1,512]{3,2,1,0:T(1,128)S(1)}, f32[2,3,1,512]{3,2,1,0:T(1,128)S(1)}, u32[]{:S(2)}, u32[]{:S(2)}) collective-permute-start(f32[2,3,1,512]{3,2,1,0:T(1,128)S(1)} %get-tuple-element.906), channel_id=1, source_target_pairs={{0,1},{1,2},{2,3},{3,4},{4,5},{5,6},{6,7},{8,9},{9,10},{10,11},{11... | collective-permute-start | bytes 36872 | tf_op jit(solution)/shard_map/while/body/eval_jaxpr/ppermute | solution.py:28
  86.3 1.9 fusion.97
  90.9 4.3 %collective-permute-start.1 = (f32[2,3,1,512]{3,2,1,0:T(1,128)S(1)}, f32[2,3,1,512]{3,2,1,0:T(1,128)S(1)}, u32[]{:S(2)}, u32[]{:S(2)}) collective-permute-start(f32[2,3,1,512]{3,2,1,0:T(1,128)S(1)} %get-tuple-element.906), channel_id=1, source_target_pairs={{0,1},{1,2},{2,3},{3,4},{4,5},{5,6},{6,7},{8,9},{9,10},{10,11},{11... | collective-permute-start | bytes 36872 | tf_op jit(solution)/shard_map/while/body/eval_jaxpr/ppermute | solution.py:28
  101.1 1.9 fusion.97
  105.7 4.3 %collective-permute-start.1 = (f32[2,3,1,512]{3,2,1,0:T(1,128)S(1)}, f32[2,3,1,512]{3,2,1,0:T(1,128)S(1)}, u32[]{:S(2)}, u32[]{:S(2)}) collective-permute-start(f32[2,3,1,512]{3,2,1,0:T(1,128)S(1)} %get-tuple-element.906), channel_id=1, source_target_pairs={{0,1},{1,2},{2,3},{3,4},{4,5},{5,6},{6,7},{8,9},{9,10},{10,11},{11... | collective-permute-start | bytes 36872 | tf_op jit(solution)/shard_map/while/body/eval_jaxpr/ppermute | solution.py:28
  115.8 1.9 fusion.97
  119.1 1.3 collective-permute-start
  120.4 4.3 %collective-permute-start.1 = (f32[2,3,1,512]{3,2,1,0:T(1,128)S(1)}, f32[2,3,1,512]{3,2,1,0:T(1,128)S(1)}, u32[]{:S(2)}, u32[]{:S(2)}) collective-permute-start(f32[2,3,1,512]{3,2,1,0:T(1,128)S(1)} %get-tuple-element.906), channel_id=1, source_target_pairs={{0,1},{1,2},{2,3},{3,4},{4,5},{5,6},{6,7},{8,9},{9,10},{10,11},{11... | collective-permute-start | bytes 36872 | tf_op jit(solution)/shard_map/while/body/eval_jaxpr/ppermute | solution.py:28
  130.6 1.9 fusion.97
  133.9 1.3 collective-permute-start
  135.2 4.3 %collective-permute-start.1 = (f32[2,3,1,512]{3,2,1,0:T(1,128)S(1)}, f32[2,3,1,512]{3,2,1,0:T(1,128)S(1)}, u32[]{:S(2)}, u32[]{:S(2)}) collective-permute-start(f32[2,3,1,512]{3,2,1,0:T(1,128)S(1)} %get-tuple-element.906), channel_id=1, source_target_pairs={{0,1},{1,2},{2,3},{3,4},{4,5},{5,6},{6,7},{8,9},{9,10},{10,11},{11... | collective-permute-start | bytes 36872 | tf_op jit(solution)/shard_map/while/body/eval_jaxpr/ppermute | solution.py:28
  145.4 1.9 fusion.97
  150.0 163.3 %while.44 = (s32[]{:T(128)}, f32[2,6,8,512]{3,2,1,0:T(8,128)S(1)}, f32[8,512]{1,0:T(8,128)S(1)}, f32[9,512]{1,0:T(8,128)S(1)}, f32[8,2,6,8,512]{4,3,2,1,0:T(8,12...) while((s32[]{:T(128)}, f32[2,6,8,512]{3,2,1,0:T(8,128)S(1)}, ...), condition=%wide.region_25.26_spmd.clone, body=%wide.region_8.25_spmd.clone.sunk | while | flops 25759636 | bytes 17506628 | solution.py:161
  157.0 2.1 fusion.114
  159.5 2.9 fusion.116
  163.3 3.6 %collective-permute-start.2 = (f32[2,3,1,512]{3,2,1,0:T(1,128)S(1)}, f32[2,3,1,512]{3,2,1,0:T(1,128)S(1)}, u32[]{:S(2)}, u32[]{:S(2)}) collective-permute-start(f32[2,3,1,512]{3,2,1,0:T(1,128)S(1)} %get-tuple-element.969), channel_id=1, source_target_pairs={{0,1},{1,2},{2,3},{3,4},{4,5},{5,6},{6,7},{8,9},{9,10},{10,11},{11... | collective-permute-start | bytes 36872 | tf_op jit(solution)/shard_map/while/body/eval_jaxpr/ppermute | solution.py:28
  167.0 1.3 collective-permute-start.3
  168.6 1.5 collective-permute-done.3
  177.3 2.1 fusion.114
  179.7 2.9 fusion.116
  183.6 3.9 %collective-permute-start.2 = (f32[2,3,1,512]{3,2,1,0:T(1,128)S(1)}, f32[2,3,1,512]{3,2,1,0:T(1,128)S(1)}, u32[]{:S(2)}, u32[]{:S(2)}) collective-permute-start(f32[2,3,1,512]{3,2,1,0:T(1,128)S(1)} %get-tuple-element.969), channel_id=1, source_target_pairs={{0,1},{1,2},{2,3},{3,4},{4,5},{5,6},{6,7},{8,9},{9,10},{10,11},{11... | collective-permute-start | bytes 36872 | tf_op jit(solution)/shard_map/while/body/eval_jaxpr/ppermute | solution.py:28
  189.0 1.5 collective-permute-done.3
  197.7 2.1 fusion.114
  200.1 2.9 fusion.116
  204.0 3.9 %collective-permute-start.2 = (f32[2,3,1,512]{3,2,1,0:T(1,128)S(1)}, f32[2,3,1,512]{3,2,1,0:T(1,128)S(1)}, u32[]{:S(2)}, u32[]{:S(2)}) collective-permute-start(f32[2,3,1,512]{3,2,1,0:T(1,128)S(1)} %get-tuple-element.969), channel_id=1, source_target_pairs={{0,1},{1,2},{2,3},{3,4},{4,5},{5,6},{6,7},{8,9},{9,10},{10,11},{11... | collective-permute-start | bytes 36872 | tf_op jit(solution)/shard_map/while/body/eval_jaxpr/ppermute | solution.py:28
  209.5 1.5 collective-permute-done.3
  218.1 2.1 fusion.114
  220.6 2.9 fusion.116
  224.4 3.9 %collective-permute-start.2 = (f32[2,3,1,512]{3,2,1,0:T(1,128)S(1)}, f32[2,3,1,512]{3,2,1,0:T(1,128)S(1)}, u32[]{:S(2)}, u32[]{:S(2)}) collective-permute-start(f32[2,3,1,512]{3,2,1,0:T(1,128)S(1)} %get-tuple-element.969), channel_id=1, source_target_pairs={{0,1},{1,2},{2,3},{3,4},{4,5},{5,6},{6,7},{8,9},{9,10},{10,11},{11... | collective-permute-start | bytes 36872 | tf_op jit(solution)/shard_map/while/body/eval_jaxpr/ppermute | solution.py:28
  228.3 1.3 collective-permute-start.3
  229.9 1.5 collective-permute-done.3
  238.6 2.1 fusion.114
  241.0 2.9 fusion.116
  244.9 3.9 %collective-permute-start.2 = (f32[2,3,1,512]{3,2,1,0:T(1,128)S(1)}, f32[2,3,1,512]{3,2,1,0:T(1,128)S(1)}, u32[]{:S(2)}, u32[]{:S(2)}) collective-permute-start(f32[2,3,1,512]{3,2,1,0:T(1,128)S(1)} %get-tuple-element.969), channel_id=1, source_target_pairs={{0,1},{1,2},{2,3},{3,4},{4,5},{5,6},{6,7},{8,9},{9,10},{10,11},{11... | collective-permute-start | bytes 36872 | tf_op jit(solution)/shard_map/while/body/eval_jaxpr/ppermute | solution.py:28
  248.8 1.3 collective-permute-start.3
  250.3 1.5 collective-permute-done.3
  259.0 2.1 fusion.114
  261.5 2.9 fusion.116
  265.3 3.9 %collective-permute-start.2 = (f32[2,3,1,512]{3,2,1,0:T(1,128)S(1)}, f32[2,3,1,512]{3,2,1,0:T(1,128)S(1)}, u32[]{:S(2)}, u32[]{:S(2)}) collective-permute-start(f32[2,3,1,512]{3,2,1,0:T(1,128)S(1)} %get-tuple-element.969), channel_id=1, source_target_pairs={{0,1},{1,2},{2,3},{3,4},{4,5},{5,6},{6,7},{8,9},{9,10},{10,11},{11... | collective-permute-start | bytes 36872 | tf_op jit(solution)/shard_map/while/body/eval_jaxpr/ppermute | solution.py:28
  270.8 1.5 collective-permute-done.3
  279.5 2.1 fusion.114
  281.9 2.9 fusion.116
  285.8 3.9 %collective-permute-start.2 = (f32[2,3,1,512]{3,2,1,0:T(1,128)S(1)}, f32[2,3,1,512]{3,2,1,0:T(1,128)S(1)}, u32[]{:S(2)}, u32[]{:S(2)}) collective-permute-start(f32[2,3,1,512]{3,2,1,0:T(1,128)S(1)} %get-tuple-element.969), channel_id=1, source_target_pairs={{0,1},{1,2},{2,3},{3,4},{4,5},{5,6},{6,7},{8,9},{9,10},{10,11},{11... | collective-permute-start | bytes 36872 | tf_op jit(solution)/shard_map/while/body/eval_jaxpr/ppermute | solution.py:28
  291.2 1.5 collective-permute-done.3
  299.9 2.1 fusion.114
  302.3 2.9 fusion.116
  306.2 3.9 %collective-permute-start.2 = (f32[2,3,1,512]{3,2,1,0:T(1,128)S(1)}, f32[2,3,1,512]{3,2,1,0:T(1,128)S(1)}, u32[]{:S(2)}, u32[]{:S(2)}) collective-permute-start(f32[2,3,1,512]{3,2,1,0:T(1,128)S(1)} %get-tuple-element.969), channel_id=1, source_target_pairs={{0,1},{1,2},{2,3},{3,4},{4,5},{5,6},{6,7},{8,9},{9,10},{10,11},{11... | collective-permute-start | bytes 36872 | tf_op jit(solution)/shard_map/while/body/eval_jaxpr/ppermute | solution.py:28
  311.7 1.5 collective-permute-done.3
  314.3 3.6 %all-to-all-start.1 = ((f32[4,2,6,8,512]{4,3,2,1,0:T(8,128)}), f32[4,2,6,8,512]{4,3,2,1,0:T(8,128)S(1)}, u32[]{:S(2)}, u32[]{:S(2)}) async-start(f32[4,2,6,8,512]{4,3,2,1,0:T(8,128)} %slice.331), calls=%async_computation.1 | async-start | bytes 1572864 | tf_op jit(solution)/shard_map/all_to_all | solution.py:168
  318.9 10.3 %all-to-all-done.1 = f32[4,2,6,8,512]{4,3,2,1,0:T(8,128)S(1)} async-done(((f32[4,2,6,8,512]{4,3,2,1,0:T(8,128)}), f32[4,2,6,8,512]{4,3,2,1,0:T(8,128)S(1)}, u32[]{:S(2)}, u32[]{:S(2)}) %all-to-all-start.1) | async-done | bytes 786464 | tf_op jit(solution)/shard_map/all_to_all | solution.py:168
  329.2 3.5 all-to-all-start
  334.0 2.0 collective-permute-done.5
  336.2 18.2 %all-reduce.15 = (f32[1,8,512]{2,1,0:T(8,128)S(1)}, f32[1,8,512]{2,1,0:T(8,128)S(1)}) all-reduce(f32[1,8,512]{2,1,0:T(8,128)S(1)} %multiply_bitcast_fusion, f32[1,8,512]{2,1,0:T(8,128)S(1)} %bitcast.178), channel_id=1, replica_groups=mesh['section'=4,'space'=8] {'section'}, use_global_device_ids=true, to_apply=%region_27.28 | all-reduce | flops 8192 | bytes 65536 | tf_op jit(solution)/shard_map/psum | solution.py:172
  (606 shorter events, 120.1 us)
Async XLA Ops:
  0.6 31.4 %copy-start.2 = (f32[3]{0:T(128)S(1)}, f32[3]{0:T(128)}, u32[]{:S(2)}) copy-start(f32[3]{0:T(128)} %constant.371.clone.1) | copy-start | bytes 40
  1.5 30.4 %collective-permute-start.4 = (f32[1,512]{1,0:T(1,128)S(1)}, f32[1,512]{1,0:T(1,128)S(1)}, u32[]{:S(2)}, u32[]{:S(2)}) collective-permute-start(f32[1,512]{1,0:T(1,128)S(1)} %slice.359), channel_id=1, source_target_pairs={{0,1},{1,2},{2,3},{3,4},{4,5},{5,6},{6,7},{8,9},{9,10},{10,11},{11... | collective-permute-start | bytes 6152 | tf_op jit(solution)/shard_map/ppermute | solution.py:18
  32.1 8.7 %collective-permute-start = (f32[2,3,1,512]{3,2,1,0:T(1,128)S(1)}, f32[2,3,1,512]{3,2,1,0:T(1,128)S(1)}, u32[]{:S(2)}, u32[]{:S(2)}) collective-permute-start(f32[2,3,1,512]{3,2,1,0:T(1,128)S(1)} %get-tuple-element.902), channel_id=1, source_target_pairs={{1,0},{2,1},{3,2},{4,3},{5,4},{6,5},{7,6},{9,8},{10,9},{11,10},{12... | collective-permute-start | bytes 36872 | tf_op jit(solution)/shard_map/while/body/eval_jaxpr/ppermute | solution.py:29
  33.4 7.4 %collective-permute-start.1 = (f32[2,3,1,512]{3,2,1,0:T(1,128)S(1)}, f32[2,3,1,512]{3,2,1,0:T(1,128)S(1)}, u32[]{:S(2)}, u32[]{:S(2)}) collective-permute-start(f32[2,3,1,512]{3,2,1,0:T(1,128)S(1)} %get-tuple-element.906), channel_id=1, source_target_pairs={{0,1},{1,2},{2,3},{3,4},{4,5},{5,6},{6,7},{8,9},{9,10},{10,11},{11... | collective-permute-start | bytes 36872 | tf_op jit(solution)/shard_map/while/body/eval_jaxpr/ppermute | solution.py:28
  45.6 9.5 %collective-permute-start = (f32[2,3,1,512]{3,2,1,0:T(1,128)S(1)}, f32[2,3,1,512]{3,2,1,0:T(1,128)S(1)}, u32[]{:S(2)}, u32[]{:S(2)}) collective-permute-start(f32[2,3,1,512]{3,2,1,0:T(1,128)S(1)} %get-tuple-element.902), channel_id=1, source_target_pairs={{1,0},{2,1},{3,2},{4,3},{5,4},{6,5},{7,6},{9,8},{10,9},{11,10},{12... | collective-permute-start | bytes 36872 | tf_op jit(solution)/shard_map/while/body/eval_jaxpr/ppermute | solution.py:29
  46.9 8.3 %collective-permute-start.1 = (f32[2,3,1,512]{3,2,1,0:T(1,128)S(1)}, f32[2,3,1,512]{3,2,1,0:T(1,128)S(1)}, u32[]{:S(2)}, u32[]{:S(2)}) collective-permute-start(f32[2,3,1,512]{3,2,1,0:T(1,128)S(1)} %get-tuple-element.906), channel_id=1, source_target_pairs={{0,1},{1,2},{2,3},{3,4},{4,5},{5,6},{6,7},{8,9},{9,10},{10,11},{11... | collective-permute-start | bytes 36872 | tf_op jit(solution)/shard_map/while/body/eval_jaxpr/ppermute | solution.py:28
  60.0 9.9 %collective-permute-start = (f32[2,3,1,512]{3,2,1,0:T(1,128)S(1)}, f32[2,3,1,512]{3,2,1,0:T(1,128)S(1)}, u32[]{:S(2)}, u32[]{:S(2)}) collective-permute-start(f32[2,3,1,512]{3,2,1,0:T(1,128)S(1)} %get-tuple-element.902), channel_id=1, source_target_pairs={{1,0},{2,1},{3,2},{4,3},{5,4},{6,5},{7,6},{9,8},{10,9},{11,10},{12... | collective-permute-start | bytes 36872 | tf_op jit(solution)/shard_map/while/body/eval_jaxpr/ppermute | solution.py:29
  61.3 8.6 %collective-permute-start.1 = (f32[2,3,1,512]{3,2,1,0:T(1,128)S(1)}, f32[2,3,1,512]{3,2,1,0:T(1,128)S(1)}, u32[]{:S(2)}, u32[]{:S(2)}) collective-permute-start(f32[2,3,1,512]{3,2,1,0:T(1,128)S(1)} %get-tuple-element.906), channel_id=1, source_target_pairs={{0,1},{1,2},{2,3},{3,4},{4,5},{5,6},{6,7},{8,9},{9,10},{10,11},{11... | collective-permute-start | bytes 36872 | tf_op jit(solution)/shard_map/while/body/eval_jaxpr/ppermute | solution.py:28
  74.8 9.9 %collective-permute-start = (f32[2,3,1,512]{3,2,1,0:T(1,128)S(1)}, f32[2,3,1,512]{3,2,1,0:T(1,128)S(1)}, u32[]{:S(2)}, u32[]{:S(2)}) collective-permute-start(f32[2,3,1,512]{3,2,1,0:T(1,128)S(1)} %get-tuple-element.902), channel_id=1, source_target_pairs={{1,0},{2,1},{3,2},{4,3},{5,4},{6,5},{7,6},{9,8},{10,9},{11,10},{12... | collective-permute-start | bytes 36872 | tf_op jit(solution)/shard_map/while/body/eval_jaxpr/ppermute | solution.py:29
  76.1 8.6 %collective-permute-start.1 = (f32[2,3,1,512]{3,2,1,0:T(1,128)S(1)}, f32[2,3,1,512]{3,2,1,0:T(1,128)S(1)}, u32[]{:S(2)}, u32[]{:S(2)}) collective-permute-start(f32[2,3,1,512]{3,2,1,0:T(1,128)S(1)} %get-tuple-element.906), channel_id=1, source_target_pairs={{0,1},{1,2},{2,3},{3,4},{4,5},{5,6},{6,7},{8,9},{9,10},{10,11},{11... | collective-permute-start | bytes 36872 | tf_op jit(solution)/shard_map/while/body/eval_jaxpr/ppermute | solution.py:28
  89.6 9.9 %collective-permute-start = (f32[2,3,1,512]{3,2,1,0:T(1,128)S(1)}, f32[2,3,1,512]{3,2,1,0:T(1,128)S(1)}, u32[]{:S(2)}, u32[]{:S(2)}) collective-permute-start(f32[2,3,1,512]{3,2,1,0:T(1,128)S(1)} %get-tuple-element.902), channel_id=1, source_target_pairs={{1,0},{2,1},{3,2},{4,3},{5,4},{6,5},{7,6},{9,8},{10,9},{11,10},{12... | collective-permute-start | bytes 36872 | tf_op jit(solution)/shard_map/while/body/eval_jaxpr/ppermute | solution.py:29
  90.9 8.6 %collective-permute-start.1 = (f32[2,3,1,512]{3,2,1,0:T(1,128)S(1)}, f32[2,3,1,512]{3,2,1,0:T(1,128)S(1)}, u32[]{:S(2)}, u32[]{:S(2)}) collective-permute-start(f32[2,3,1,512]{3,2,1,0:T(1,128)S(1)} %get-tuple-element.906), channel_id=1, source_target_pairs={{0,1},{1,2},{2,3},{3,4},{4,5},{5,6},{6,7},{8,9},{9,10},{10,11},{11... | collective-permute-start | bytes 36872 | tf_op jit(solution)/shard_map/while/body/eval_jaxpr/ppermute | solution.py:28
  104.4 9.9 %collective-permute-start = (f32[2,3,1,512]{3,2,1,0:T(1,128)S(1)}, f32[2,3,1,512]{3,2,1,0:T(1,128)S(1)}, u32[]{:S(2)}, u32[]{:S(2)}) collective-permute-start(f32[2,3,1,512]{3,2,1,0:T(1,128)S(1)} %get-tuple-element.902), channel_id=1, source_target_pairs={{1,0},{2,1},{3,2},{4,3},{5,4},{6,5},{7,6},{9,8},{10,9},{11,10},{12... | collective-permute-start | bytes 36872 | tf_op jit(solution)/shard_map/while/body/eval_jaxpr/ppermute | solution.py:29
  105.7 8.6 %collective-permute-start.1 = (f32[2,3,1,512]{3,2,1,0:T(1,128)S(1)}, f32[2,3,1,512]{3,2,1,0:T(1,128)S(1)}, u32[]{:S(2)}, u32[]{:S(2)}) collective-permute-start(f32[2,3,1,512]{3,2,1,0:T(1,128)S(1)} %get-tuple-element.906), channel_id=1, source_target_pairs={{0,1},{1,2},{2,3},{3,4},{4,5},{5,6},{6,7},{8,9},{9,10},{10,11},{11... | collective-permute-start | bytes 36872 | tf_op jit(solution)/shard_map/while/body/eval_jaxpr/ppermute | solution.py:28
  119.1 9.9 %collective-permute-start = (f32[2,3,1,512]{3,2,1,0:T(1,128)S(1)}, f32[2,3,1,512]{3,2,1,0:T(1,128)S(1)}, u32[]{:S(2)}, u32[]{:S(2)}) collective-permute-start(f32[2,3,1,512]{3,2,1,0:T(1,128)S(1)} %get-tuple-element.902), channel_id=1, source_target_pairs={{1,0},{2,1},{3,2},{4,3},{5,4},{6,5},{7,6},{9,8},{10,9},{11,10},{12... | collective-permute-start | bytes 36872 | tf_op jit(solution)/shard_map/while/body/eval_jaxpr/ppermute | solution.py:29
  120.4 8.6 %collective-permute-start.1 = (f32[2,3,1,512]{3,2,1,0:T(1,128)S(1)}, f32[2,3,1,512]{3,2,1,0:T(1,128)S(1)}, u32[]{:S(2)}, u32[]{:S(2)}) collective-permute-start(f32[2,3,1,512]{3,2,1,0:T(1,128)S(1)} %get-tuple-element.906), channel_id=1, source_target_pairs={{0,1},{1,2},{2,3},{3,4},{4,5},{5,6},{6,7},{8,9},{9,10},{10,11},{11... | collective-permute-start | bytes 36872 | tf_op jit(solution)/shard_map/while/body/eval_jaxpr/ppermute | solution.py:28
  133.9 9.9 %collective-permute-start = (f32[2,3,1,512]{3,2,1,0:T(1,128)S(1)}, f32[2,3,1,512]{3,2,1,0:T(1,128)S(1)}, u32[]{:S(2)}, u32[]{:S(2)}) collective-permute-start(f32[2,3,1,512]{3,2,1,0:T(1,128)S(1)} %get-tuple-element.902), channel_id=1, source_target_pairs={{1,0},{2,1},{3,2},{4,3},{5,4},{6,5},{7,6},{9,8},{10,9},{11,10},{12... | collective-permute-start | bytes 36872 | tf_op jit(solution)/shard_map/while/body/eval_jaxpr/ppermute | solution.py:29
  135.2 8.6 %collective-permute-start.1 = (f32[2,3,1,512]{3,2,1,0:T(1,128)S(1)}, f32[2,3,1,512]{3,2,1,0:T(1,128)S(1)}, u32[]{:S(2)}, u32[]{:S(2)}) collective-permute-start(f32[2,3,1,512]{3,2,1,0:T(1,128)S(1)} %get-tuple-element.906), channel_id=1, source_target_pairs={{0,1},{1,2},{2,3},{3,4},{4,5},{5,6},{6,7},{8,9},{9,10},{10,11},{11... | collective-permute-start | bytes 36872 | tf_op jit(solution)/shard_map/while/body/eval_jaxpr/ppermute | solution.py:28
  148.7 1.1 copy-start
  163.3 5.1 %collective-permute-start.2 = (f32[2,3,1,512]{3,2,1,0:T(1,128)S(1)}, f32[2,3,1,512]{3,2,1,0:T(1,128)S(1)}, u32[]{:S(2)}, u32[]{:S(2)}) collective-permute-start(f32[2,3,1,512]{3,2,1,0:T(1,128)S(1)} %get-tuple-element.969), channel_id=1, source_target_pairs={{0,1},{1,2},{2,3},{3,4},{4,5},{5,6},{6,7},{8,9},{9,10},{10,11},{11... | collective-permute-start | bytes 36872 | tf_op jit(solution)/shard_map/while/body/eval_jaxpr/ppermute | solution.py:28
  167.0 3.1 collective-permute-start.3
  183.6 5.3 %collective-permute-start.2 = (f32[2,3,1,512]{3,2,1,0:T(1,128)S(1)}, f32[2,3,1,512]{3,2,1,0:T(1,128)S(1)}, u32[]{:S(2)}, u32[]{:S(2)}) collective-permute-start(f32[2,3,1,512]{3,2,1,0:T(1,128)S(1)} %get-tuple-element.969), channel_id=1, source_target_pairs={{0,1},{1,2},{2,3},{3,4},{4,5},{5,6},{6,7},{8,9},{9,10},{10,11},{11... | collective-permute-start | bytes 36872 | tf_op jit(solution)/shard_map/while/body/eval_jaxpr/ppermute | solution.py:28
  187.4 3.1 collective-permute-start.3
  204.0 5.3 %collective-permute-start.2 = (f32[2,3,1,512]{3,2,1,0:T(1,128)S(1)}, f32[2,3,1,512]{3,2,1,0:T(1,128)S(1)}, u32[]{:S(2)}, u32[]{:S(2)}) collective-permute-start(f32[2,3,1,512]{3,2,1,0:T(1,128)S(1)} %get-tuple-element.969), channel_id=1, source_target_pairs={{0,1},{1,2},{2,3},{3,4},{4,5},{5,6},{6,7},{8,9},{9,10},{10,11},{11... | collective-permute-start | bytes 36872 | tf_op jit(solution)/shard_map/while/body/eval_jaxpr/ppermute | solution.py:28
  207.9 3.1 collective-permute-start.3
  224.4 5.3 %collective-permute-start.2 = (f32[2,3,1,512]{3,2,1,0:T(1,128)S(1)}, f32[2,3,1,512]{3,2,1,0:T(1,128)S(1)}, u32[]{:S(2)}, u32[]{:S(2)}) collective-permute-start(f32[2,3,1,512]{3,2,1,0:T(1,128)S(1)} %get-tuple-element.969), channel_id=1, source_target_pairs={{0,1},{1,2},{2,3},{3,4},{4,5},{5,6},{6,7},{8,9},{9,10},{10,11},{11... | collective-permute-start | bytes 36872 | tf_op jit(solution)/shard_map/while/body/eval_jaxpr/ppermute | solution.py:28
  228.3 3.1 collective-permute-start.3
  244.9 5.3 %collective-permute-start.2 = (f32[2,3,1,512]{3,2,1,0:T(1,128)S(1)}, f32[2,3,1,512]{3,2,1,0:T(1,128)S(1)}, u32[]{:S(2)}, u32[]{:S(2)}) collective-permute-start(f32[2,3,1,512]{3,2,1,0:T(1,128)S(1)} %get-tuple-element.969), channel_id=1, source_target_pairs={{0,1},{1,2},{2,3},{3,4},{4,5},{5,6},{6,7},{8,9},{9,10},{10,11},{11... | collective-permute-start | bytes 36872 | tf_op jit(solution)/shard_map/while/body/eval_jaxpr/ppermute | solution.py:28
  248.8 3.1 collective-permute-start.3
  265.3 5.3 %collective-permute-start.2 = (f32[2,3,1,512]{3,2,1,0:T(1,128)S(1)}, f32[2,3,1,512]{3,2,1,0:T(1,128)S(1)}, u32[]{:S(2)}, u32[]{:S(2)}) collective-permute-start(f32[2,3,1,512]{3,2,1,0:T(1,128)S(1)} %get-tuple-element.969), channel_id=1, source_target_pairs={{0,1},{1,2},{2,3},{3,4},{4,5},{5,6},{6,7},{8,9},{9,10},{10,11},{11... | collective-permute-start | bytes 36872 | tf_op jit(solution)/shard_map/while/body/eval_jaxpr/ppermute | solution.py:28
  269.2 3.1 collective-permute-start.3
  285.8 5.3 %collective-permute-start.2 = (f32[2,3,1,512]{3,2,1,0:T(1,128)S(1)}, f32[2,3,1,512]{3,2,1,0:T(1,128)S(1)}, u32[]{:S(2)}, u32[]{:S(2)}) collective-permute-start(f32[2,3,1,512]{3,2,1,0:T(1,128)S(1)} %get-tuple-element.969), channel_id=1, source_target_pairs={{0,1},{1,2},{2,3},{3,4},{4,5},{5,6},{6,7},{8,9},{9,10},{10,11},{11... | collective-permute-start | bytes 36872 | tf_op jit(solution)/shard_map/while/body/eval_jaxpr/ppermute | solution.py:28
  289.7 3.1 collective-permute-start.3
  306.2 5.3 %collective-permute-start.2 = (f32[2,3,1,512]{3,2,1,0:T(1,128)S(1)}, f32[2,3,1,512]{3,2,1,0:T(1,128)S(1)}, u32[]{:S(2)}, u32[]{:S(2)}) collective-permute-start(f32[2,3,1,512]{3,2,1,0:T(1,128)S(1)} %get-tuple-element.969), channel_id=1, source_target_pairs={{0,1},{1,2},{2,3},{3,4},{4,5},{5,6},{6,7},{8,9},{9,10},{10,11},{11... | collective-permute-start | bytes 36872 | tf_op jit(solution)/shard_map/while/body/eval_jaxpr/ppermute | solution.py:28
  310.1 3.1 collective-permute-start.3
  314.3 3.6 %copy-start.1 = (f32[8,2,6,8,512]{4,3,2,1,0:T(8,128)S(1)}, f32[8,2,6,8,512]{4,3,2,1,0:T(8,128)}, u32[]{:S(2)}) copy-start(f32[8,2,6,8,512]{4,3,2,1,0:T(8,128)} %copy-done) | copy-start | bytes 4718596
  314.3 14.9 %all-to-all-start.1 = ((f32[4,2,6,8,512]{4,3,2,1,0:T(8,128)}), f32[4,2,6,8,512]{4,3,2,1,0:T(8,128)S(1)}, u32[]{:S(2)}, u32[]{:S(2)}) async-start(f32[4,2,6,8,512]{4,3,2,1,0:T(8,128)} %slice.331), calls=%async_computation.1 | async-start | bytes 1572864 | tf_op jit(solution)/shard_map/all_to_all | solution.py:168
  329.2 25.8 %all-to-all-start = ((f32[4,2,6,8,512]{4,3,2,1,0:T(8,128)}), f32[4,2,6,8,512]{4,3,2,1,0:T(8,128)S(1)}, u32[]{:S(2)}, u32[]{:S(2)}) async-start(f32[4,2,6,8,512]{4,3,2,1,0:T(8,128)} %slice.330), calls=%async_computation | async-start | bytes 1572864 | tf_op jit(solution)/shard_map/all_to_all | solution.py:167
  332.7 3.3 collective-permute-start.5
where the time goes:
time: 359 us; the launch traced here: 357 us
  starting transfers between devices  94.8 us (26%)
  other arithmetic  94.1 us (26%)
  local copies, waits for them, and re-layouts  49.9 us (14%)
  blocking collectives  41.7 us (12%)
  loops' own time  34.8 us (10%)
  waiting for transfers between devices  24.3 us (7%)
  matrix products  15.6 us (4%)
    ppermute x16, starting transfers between devices, padded(): before = lax.ppermute(last, axis, up)  63.3 us
    reduce_sum x16, other arithmetic, contact(): jnp.sum(separation * separation, axis=0)  25 us
    reduce_sum x8, other arithmetic, contact(): separation = own_points[:, :, :, None] - other_points[:, :, None, :]  23.2 us
    ppermute x16, starting transfers between devices, padded(): after = lax.ppermute(first, axis, down)  20.7 us
    psum x1, blocking collectives, on_device(): summed_row, summed_column = lax.psum((grad_row, column_own), 'section')  18.2 us
    another operation x1, loops' own time, on_device(): lax.scan(backward_step, start_carry, (numbers, extended_all, velocity_all...  17.9 us
    another operation x1, loops' own time, on_device(): lax.scan(forward_step, own_start, numbers)  17 us
    reduce_sum x8, other arithmetic, contact(): jnp.sum(spring_weights[None] * separation, axis=3)  15.4 us
  transfers between devices with their start and end apart: 36, of which 10 were waited for; matrix products, arithmetic and copies ran while one was open for 7% of the time, Pallas kernels for 0%

commit v1 on v0

v1 whole, which is shorter than its diff:
```python
import functools

import jax
import jax.numpy as jnp
from jax import lax
from jax.experimental import pallas as pl
from jax.experimental.pallas import tpu as pltpu
from jax.sharding import PartitionSpec as P

time_step = 0.1
damping = 0.98
contact_scale = 0.3
kernel_spread = 2.0
gravity = 0.5
tiny_length = 1e-06
LANES = 128
CHUNK = 32
MESH = pl.DeviceIdType.MESH


def total(parts):
    result = parts[0]
    for part in parts[1:]:
        result = result + part
    return result


def kernel(
    dims,
    start_hbm,
    stiff_ref,
    lists_ref,
    cot_hbm,
    exit_hbm,
    adj_hbm,
    grad_ref,
    lists_all,
    lists_s,
    ext,
    vel,
    adj,
    exit_buf,
    adj_buf,
    halo_out,
    halo_in,
    back_out,
    back_in,
    above_out,
    above_in,
    upper_out,
    upper_in,
    grad_parts,
    gath,
    force_adj,
    load_sem,
    smem_sem,
    list_send,
    list_recv,
    halo_send,
    halo_recv,
    back_send,
    back_recv,
    above_send,
    above_recv,
    upper_send,
    upper_recv,
    exit_send,
    exit_recv,
    adj_send,
    adj_recv,
    grad_send,
    grad_recv,
):
    sections, spaces, share, steps_section, pairs, rows, width = dims
    steps = sections * steps_section
    quarter = width // LANES
    sec = lax.axis_index("section")
    spc = lax.axis_index("space")
    has_up = spc > 0
    has_down = spc < spaces - 1

    row_id = lax.broadcasted_iota(jnp.int32, (rows, width), 0)
    lane_id = lax.broadcasted_iota(jnp.int32, (rows, width), 1)
    tile_in_row = lax.shift_right_logical(lane_id, LANES.bit_length() - 1)
    tile_id = row_id * quarter + tile_in_row
    first_row = row_id == 0
    last_row = row_id == rows - 1
    halo_tile = jnp.where(
        first_row,
        tile_in_row,
        jnp.where(row_id == 1, tile_in_row + (rows + 1) * quarter, -1),
    )

    def remote(src, dst, send, recv, device):
        return pltpu.make_async_remote_copy(
            src_ref=src,
            dst_ref=dst,
            send_sem=send,
            recv_sem=recv,
            device_id=device,
            device_id_type=MESH,
        )

    def peer(k):
        return lax.rem(sec + k, sections)

    def store_rows(ref, index, row, value):
        for q in range(quarter):
            part = value[:, q * LANES : (q + 1) * LANES]
            ref[index + (q, slice(row, row + value.shape[0]), slice(None))] = part

    def load_rows(ref, index, row, count):
        parts = [ref[index + (q, slice(row, row + count), slice(None))] for q in range(quarter)]
        return jnp.concatenate(parts, axis=1)

    loads = []
    for t in range(share):
        for c in range(3):
            loads.append(
                pltpu.make_async_copy(
                    start_hbm.at[sec * share + t, c],
                    exit_buf.at[0, t, c],
                    load_sem.at[0, t, c],
                )
            )
        loads.append(
            pltpu.make_async_copy(
                start_hbm.at[sec * share + t, pl.ds(3, 3)], vel.at[t], load_sem.at[1, t, 0]
            )
        )
        loads.append(
            pltpu.make_async_copy(cot_hbm.at[sec * share + t], adj.at[t], load_sem.at[1, t, 1])
        )
    for copy in loads:
        copy.start()

    above_out[...] = stiff_ref[1, rows - 1 : rows, :]
    above_in[...] = jnp.zeros_like(above_in)
    upper_in[...] = jnp.zeros_like(upper_in)
    halo_in[...] = jnp.zeros_like(halo_in)
    back_in[...] = jnp.zeros_like(back_in)
    gath[...] = jnp.zeros_like(gath)
    lists_all[sec] = lists_ref[...]
    barrier = pltpu.get_barrier_semaphore()
    for k in range(1, sections):
        pl.semaphore_signal(barrier, inc=1, device_id=(peer(k), spc), device_id_type=MESH)

    @pl.when(has_up)
    def _():
        pl.semaphore_signal(barrier, inc=1, device_id=(sec, spc - 1), device_id_type=MESH)

    @pl.when(has_down)
    def _():
        pl.semaphore_signal(barrier, inc=1, device_id=(sec, spc + 1), device_id_type=MESH)

    for copy in loads:
        copy.wait()
    for t in range(share):
        for c in range(3):
            now = exit_buf[0, t, c]
            store_rows(ext, (0, t, c), 0, now)
            halo_out[0, t, 0, c : c + 1, :] = now[0:1]
            halo_out[0, t, 1, c : c + 1, :] = now[rows - 1 : rows]

    greeted = jnp.where(has_up, 1, 0) + jnp.where(has_down, 1, 0)
    pl.semaphore_wait(barrier, sections - 1 + greeted)

    def to_up(out, into, send, recv, g, t):
        return remote(
            out.at[g, t, 0], into.at[g, t, 1], send.at[g, t, 0], recv.at[g, t, 1], (sec, spc - 1)
        )

    def to_down(out, into, send, recv, g, t):
        return remote(
            out.at[g, t, 1], into.at[g, t, 0], send.at[g, t, 1], recv.at[g, t, 0], (sec, spc + 1)
        )

    halo = (halo_out, halo_in, halo_send, halo_recv)
    back = (back_out, back_in, back_send, back_recv)

    def exchange(kind, g, t):
        @pl.when(has_up)
        def _():
            to_up(*kind, g, t).start()

        @pl.when(has_down)
        def _():
            to_down(*kind, g, t).start()

    def arrive(kind, g, t):
        out, into, send, recv = kind

        @pl.when(has_up)
        def _():
            remote(
                out.at[g, t, 1], into.at[g, t, 0], send.at[g, t, 1], recv.at[g, t, 0], (sec, spc - 1)
            ).wait_recv()

        @pl.when(has_down)
        def _():
            remote(
                out.at[g, t, 0], into.at[g, t, 1], send.at[g, t, 0], recv.at[g, t, 1], (sec, spc + 1)
            ).wait_recv()

    def sent(kind, g, t):
        @pl.when(has_up)
        def _():
            to_up(*kind, g, t).wait_send()

        @pl.when(has_down)
        def _():
            to_down(*kind, g, t).wait_send()

    list_copies = [
        remote(
            lists_ref,
            lists_all.at[sec],
            list_send.at[k - 1],
            list_recv.at[k - 1],
            (peer(k), spc),
        )
        for k in range(1, sections)
    ]
    for copy in list_copies:
        copy.start()
    for t in range(share):
        exchange(halo, 0, t)

    def above_copy():
        return remote(above_out, above_in, above_send, above_recv, (sec, spc + 1))

    @pl.when(has_down)
    def _():
        above_copy().start()

    for copy in list_copies:
        copy.wait()
    to_scalar = pltpu.make_async_copy(lists_all, lists_s, smem_sem)
    to_scalar.start()
    to_scalar.wait()

    @pl.when(has_down)
    def _():
        above_copy().wait_send()

    @pl.when(has_up)
    def _():
        remote(above_out, above_in, above_send, above_recv, (sec, spc - 1)).wait_recv()

    column_mask = (lane_id < width - 1).astype(jnp.float32)
    row_mask = jnp.where(
        jnp.logical_and(last_row, spc * rows + row_id == spaces * rows - 1), 0.0, 1.0
    )

    def right_of(value):
        return pltpu.roll(value, width - 1, 1)

    def left_of(value):
        return pltpu.roll(value, 1, 1)

    def below(value):
        return pltpu.roll(value, rows - 1, 0)

    def above(value):
        return pltpu.roll(value, 1, 0)

    def square(d):
        return d[0] * d[0] + d[1] * d[1] + d[2] * d[2]

    def contact_slot(g, t, p):
        ordinal = g // steps_section
        inner = lax.rem(g, steps_section)
        first = lists_s[ordinal, inner, p]
        second = lists_s[ordinal, inner, pairs + p]
        live = jnp.where(p < lists_s[ordinal, inner, 2 * pairs], 1.0, 0.0)
        return first, second, live

    def tile_rows(ref, index, row, column):
        return [
            ref[index + (c, column, pl.ds(row, 1), slice(None))]
            for c in range(3)
        ]

    def gather_others(g, t):
        for p in range(pairs):
            _, second, _ = contact_slot(g, t, p)
            row = second // quarter
            column = lax.rem(second, quarter)
            place = jnp.where(
                row == 0, rows, jnp.where(row == rows + 1, rows + 1, row - 1)
            )
            found = tile_rows(ext, (g, t), place, column)
            for c in range(3):
                gath[4 * p + c : 4 * p + c + 1, :] = found[c]
        return gath[...].T

    def wide(value):
        return jnp.concatenate([value] * quarter, axis=1)

    coefficient = 2.0 * contact_scale / kernel_spread

    def forward_one(g, t):
        arrive(halo, g, t)
        for side in range(2):
            for c in range(3):
                store_rows(ext, (g, t, c), rows + side, halo_in[g, t, side, c : c + 1, :])
        x = [load_rows(ext, (g, t, c), 0, rows) for c in range(3)]
        up = [load_rows(ext, (g, t, c), rows, 1) for c in range(3)]
        down = [load_rows(ext, (g, t, c), rows + 1, 1) for c in range(3)]
        k_row = stiff_ref[0] * column_mask
        k_column = stiff_ref[1] * row_mask
        d = [right_of(v) - v for v in x]
        pull = k_row * (1.0 - lax.rsqrt(square(d) + tiny_length))
        pulls = [pull * v for v in d]
        force = [v - left_of(v) for v in pulls]
        d = [jnp.where(last_row, down[c], below(x[c])) - x[c] for c in range(3)]
        pull = k_column * (1.0 - lax.rsqrt(square(d) + tiny_length))
        pulls = [pull * v for v in d]
        d = [up[c] - x[c][0:1] for c in range(3)]
        pull = above_in[...] * (1.0 - lax.rsqrt(square(d) + tiny_length))
        force = [
            force[c] + pulls[c] + jnp.where(first_row, pull * d[c], -above(pulls[c]))
            for c in range(3)
        ]
        columns = gather_others(g, t)
        for p in range(pairs):
            first, _, live = contact_slot(g, t, p)
            own = tile_rows(ext, (g, t), first // quarter, lax.rem(first, quarter))
            sums = None
            for j in range(0, LANES, CHUNK):
                s = [own[c] - columns[j : j + CHUNK, 4 * p + c : 4 * p + c + 1] for c in range(3)]
                weight = jnp.exp(square(s) * (-1.0 / kernel_spread))
                terms = [weight * v for v in s]
                sums = terms if sums is None else [a + b for a, b in zip(sums, terms)]
            here = tile_id == first
            for c in range(3):
                repulsion = (coefficient * live) * jnp.sum(sums[c], axis=0, keepdims=True)
                force[c] = force[c] + jnp.where(here, wide(repulsion), 0.0)
        force[2] = force[2] - gravity
        ordinal = g // steps_section
        leaving = lax.rem(g, steps_section) == steps_section - 1
        for c in range(3):
            moved = damping * (vel[t, c] + time_step * force[c])
            point = x[c] + time_step * moved
            vel[t, c] = moved
            store_rows(ext, (g + 1, t, c), 0, point)
            halo_out[g + 1, t, 0, c : c + 1, :] = point[0:1]
            halo_out[g + 1, t, 1, c : c + 1, :] = point[rows - 1 : rows]
            exit_buf[ordinal, t, c] = point
            exit_buf[ordinal, t, 3 + c] = moved

        @pl.when(g < steps - 1)
        def _():
            exchange(halo, g + 1, t)

        @pl.when(leaving)
        def _():
            deliver(exit_buf, exit_hbm, exit_send, exit_recv, 0, ordinal, t, 0, 6)

    def deliver(buf, hbm, send, recv, part, ordinal, t, low, count):
        source = buf.at[ordinal, t, pl.ds(low, count)]
        target = hbm.at[0, sec * share + t, pl.ds(low, count)]

        @pl.when(ordinal == sec)
        def _():
            pltpu.make_async_copy(source, target, send.at[ordinal, t, part]).start()

        @pl.when(ordinal != sec)
        def _():
            remote(
                source, target, send.at[ordinal, t, part], recv.at[sec, t, part], (ordinal, spc)
            ).start()

    def delivered(buf, hbm, send, recv, part, t, low, count):
        for k in range(sections):
            source = buf.at[k, t, pl.ds(low, count)]
            target = hbm.at[0, k * share + t, pl.ds(low, count)]

            @pl.when(sec == k)
            def _():
                pltpu.make_async_copy(source, target, send.at[k, t, part]).wait()

            @pl.when(sec != k)
            def _():
                copy = remote(source, target, send.at[k, t, part], recv.at[k, t, part], (k, spc))
                copy.wait_send()
                copy.wait_recv()

    def forward_step(g, carry):
        for t in range(share):
            forward_one(g, t)
        return carry

    lax.fori_loop(0, steps, forward_step, 0)

    def finish(g, t):
        arrive(back, g, t)
        for c in range(3):
            value = adj[t, c]
            value = value + jnp.where(
                first_row,
                back_in[g, t, 0, c : c + 1, :],
                jnp.where(last_row, back_in[g, t, 1, c : c + 1, :], 0.0),
            )
            adj[t, c] = value
            adj_buf[g // steps_section, t, c] = value

        @pl.when(lax.rem(g, steps_section) == 0)
        def _():
            deliver(adj_buf, adj_hbm, adj_send, adj_recv, 0, g // steps_section, t, 0, 3)

    def back_one(g, t, grads):
        grad_row, grad_column, grad_upper = grads

        @pl.when(g < steps - 1)
        def _():
            finish(g + 1, t)

        point_adj = [adj[t, c] for c in range(3)]
        f = []
        ordinal = g // steps_section
        for c in range(3):
            passed = damping * (adj[t, 3 + c] + time_step * point_adj[c])
            adj[t, 3 + c] = passed
            adj_buf[ordinal, t, 3 + c] = passed
            f.append(time_step * passed)
        for c in range(3):
            store_rows(force_adj, (t, c), 0, f[c])

        @pl.when(lax.rem(g, steps_section) == 0)
        def _():
            deliver(adj_buf, adj_hbm, adj_send, adj_recv, 1, ordinal, t, 3, 3)

        x = [load_rows(ext, (g, t, c), 0, rows) for c in range(3)]
        up = [load_rows(ext, (g, t, c), rows, 1) for c in range(3)]
        down = [load_rows(ext, (g, t, c), rows + 1, 1) for c in range(3)]

        def edge(d, phi, constant):
            inverse = lax.rsqrt(square(d) + tiny_length)
            bend = 1.0 - inverse
            along = d[0] * phi[0] + d[1] * phi[1] + d[2] * phi[2]
            twist = inverse * inverse * inverse * along
            return bend * along, [constant * (bend * phi[c] + twist * d[c]) for c in range(3)]

        d = [right_of(v) - v for v in x]
        part, offset = edge(d, [v - right_of(v) for v in f], stiff_ref[0] * column_mask)
        grad_row = grad_row + part
        out = [point_adj[c] - offset[c] + left_of(offset[c]) for c in range(3)]
        d = [jnp.where(last_row, down[c], below(x[c])) - x[c] for c in range(3)]
        phi = [v - jnp.where(last_row, 0.0, below(v)) for v in f]
        part, offset = edge(d, phi, stiff_ref[1] * row_mask)
        grad_column = grad_column + part
        down_adj = [offset[c][rows - 1 : rows] for c in range(3)]
        d = [up[c] - x[c][0:1] for c in range(3)]
        part, up_adj = edge(d, [v[0:1] for v in f], above_in[...])
        grad_upper = grad_upper + part
        out = [
            out[c] - offset[c] + jnp.where(first_row, -up_adj[c], above(offset[c]))
            for c in range(3)
        ]
        columns = gather_others(g, t)
        ghost = [jnp.zeros((rows, width), jnp.float32) for _ in range(3)]
        for p in range(pairs):
            first, second, live = contact_slot(g, t, p)
            row, column = first // quarter, lax.rem(first, quarter)
            own = tile_rows(ext, (g, t), row, column)
            scale = coefficient * live
            pulled = [scale * v for v in tile_rows(force_adj, (t,), row, column)]
            sums = None
            across = []
            for j in range(0, LANES, CHUNK):
                s = [own[c] - columns[j : j + CHUNK, 4 * p + c : 4 * p + c + 1] for c in range(3)]
                weight = jnp.exp(square(s) * (-1.0 / kernel_spread))
                along = s[0] * pulled[0] + s[1] * pulled[1] + s[2] * pulled[2]
                terms = [weight * (pulled[c] - along * s[c]) for c in range(3)]
                sums = terms if sums is None else [a + b for a, b in zip(sums, terms)]
                across.append([jnp.sum(v, axis=1, keepdims=True) for v in terms])
            here = tile_id == first
            there = tile_id == second - quarter
            outside = halo_tile == second
            for c in range(3):
                gain = wide(jnp.sum(sums[c], axis=0, keepdims=True))
                loss = jnp.concatenate([a[c] for a in across], axis=0)
                loss = wide(jnp.broadcast_to(loss, (LANES, 8)).T[0:1])
                out[c] = out[c] + jnp.where(here, gain, 0.0) - jnp.where(there, loss, 0.0)
                ghost[c] = ghost[c] - jnp.where(outside, loss, 0.0)
        for c in range(3):
            adj[t, c] = out[c]
            back_out[g, t, 0, c : c + 1, :] = up_adj[c] + ghost[c][0:1]
            back_out[g, t, 1, c : c + 1, :] = down_adj[c] + ghost[c][1:2]
        exchange(back, g, t)
        return grad_row, grad_column, grad_upper

    def back_step(i, grads):
        for t in range(share):
            grads = back_one(steps - 1 - i, t, grads)
        return grads

    zero = jnp.zeros((rows, width), jnp.float32)
    grad_row, grad_column, grad_upper = lax.fori_loop(
        0, steps, back_step, (zero, zero, jnp.zeros((1, width), jnp.float32))
    )

    upper_out[...] = grad_upper

    def upper_copy(to):
        return remote(upper_out, upper_in, upper_send, upper_recv, (sec, to))

    @pl.when(has_up)
    def _():
        upper_copy(spc - 1).start()

    @pl.when(has_down)
    def _():
        upper_copy(spc + 1).wait_recv()

    grad_column = grad_column + jnp.where(last_row, upper_in[...], 0.0)
    grad_parts[sec, 0] = grad_row * column_mask
    grad_parts[sec, 1] = grad_column * row_mask
    grad_copies = [
        remote(
            grad_parts.at[sec],
            grad_parts.at[sec],
            grad_send.at[k - 1],
            grad_recv.at[k - 1],
            (peer(k), spc),
        )
        for k in range(1, sections)
    ]
    for copy in grad_copies:
        copy.start()
    for t in range(share):
        finish(0, t)
    for k in range(1, sections):
        other = lax.rem(sec + sections - k, sections)
        remote(
            grad_parts.at[sec],
            grad_parts.at[other],
            grad_send.at[k - 1],
            grad_recv.at[k - 1],
            (peer(k), spc),
        ).wait()
    for c in range(2):
        grad_ref[c] = total([grad_parts[k, c] for k in range(sections)])

    @pl.when(has_up)
    def _():
        upper_copy(spc - 1).wait_send()

    def drain(g, carry):
        for t in range(share):
            sent(halo, g, t)
            sent(back, g, t)
        return carry

    lax.fori_loop(0, steps, drain, 0)
    for t in range(share):
        delivered(exit_buf, exit_hbm, exit_send, exit_recv, 0, t, 0, 6)
        delivered(adj_buf, adj_hbm, adj_send, adj_recv, 1, t, 3, 3)
        delivered(adj_buf, adj_hbm, adj_send, adj_recv, 0, t, 0, 3)


def on_device(start_state, stiffness, contact_a, contact_b, pair_count, cotangent):
    sections, spaces = lax.axis_size("section"), lax.axis_size("space")
    micro, parts, rows, width = start_state.shape
    steps_section, _, pairs = contact_a.shape
    share = micro // sections
    steps = sections * steps_section
    lists = jnp.concatenate([contact_a[:, 0], contact_b[:, 0], pair_count], axis=1)
    lists = jnp.pad(lists, ((0, 8 - steps_section), (0, LANES - lists.shape[1])))
    dims = (sections, spaces, share, steps_section, pairs, rows, width)
    dma = pltpu.SemaphoreType.DMA
    f32 = jnp.float32
    out_state = jax.ShapeDtypeStruct((1, micro, parts, rows, width), f32)
    anywhere = pl.BlockSpec(memory_space=pl.ANY)
    vmem = pl.BlockSpec(memory_space=pltpu.VMEM)
    return pl.pallas_call(
        functools.partial(kernel, dims),
        out_shape=(out_state, out_state, jax.ShapeDtypeStruct((2, rows, width), f32)),
        in_specs=[anywhere, vmem, vmem, anywhere],
        out_specs=(anywhere, anywhere, vmem),
        scratch_shapes=[
            pltpu.VMEM((sections, 8, LANES), jnp.int32),
            pltpu.SMEM((sections, 8, LANES), jnp.int32),
            pltpu.VMEM((steps + 1, share, 3, width // LANES, 2 * rows, LANES), f32),
            pltpu.VMEM((share, 3, rows, width), f32),
            pltpu.VMEM((share, parts, rows, width), f32),
            pltpu.VMEM((sections, share, parts, rows, width), f32),
            pltpu.VMEM((sections, share, parts, rows, width), f32),
            pltpu.VMEM((steps + 1, share, 2, 3, width), f32),
            pltpu.VMEM((steps, share, 2, 3, width), f32),
            pltpu.VMEM((steps, share, 2, 3, width), f32),
            pltpu.VMEM((steps, share, 2, 3, width), f32),
            pltpu.VMEM((1, width), f32),
            pltpu.VMEM((1, width), f32),
            pltpu.VMEM((1, width), f32),
            pltpu.VMEM((1, width), f32),
            pltpu.VMEM((sections, 2, rows, width), f32),
            pltpu.VMEM((LANES, LANES), f32),
            pltpu.VMEM((share, 3, width // LANES, rows, LANES), f32),
            dma((2, share, 3)),
            dma,
            dma((sections - 1,)),
            dma((sections - 1,)),
            dma((steps, share, 2)),
            dma((steps, share, 2)),
            dma((steps, share, 2)),
            dma((steps, share, 2)),
            dma,
            dma,
            dma,
            dma,
            dma((sections, share, 1)),
            dma((sections, share, 1)),
            dma((sections, share, 2)),
            dma((sections, share, 2)),
            dma((sections - 1,)),
            dma((sections - 1,)),
        ],
        compiler_params=pltpu.CompilerParams(collective_id=0, has_side_effects=True),
    )(start_state, stiffness, lists, cotangent)


def solution(mesh):
    in_specs = (
        P(None, None, "space", None),
        P(None, "space", None),
        P("section", "space", None),
        P("section", "space", None),
        P("section", "space"),
        P(None, None, "space", None),
    )
    out_specs = (
        P("section", None, None, "space", None),
        P("section", None, None, "space", None),
        P(None, "space", None),
    )
    return jax.shard_map(
        on_device, mesh=mesh, in_specs=in_specs, out_specs=out_specs, check_vma=False
    )
```

time: 359 us -> 129 us (0.36)
  Pallas kernels: 0 us -> 122 us
  starting transfers between devices: 94.8 us -> 0 us
  other arithmetic: 94.1 us -> 0.07 us
  local copies, waits for them, and re-layouts: 49.9 us -> 5.56 us
  blocking collectives: 41.7 us -> 0 us
  loops' own time: 34.8 us -> 0 us
  waiting for transfers between devices: 24.3 us -> 0 us
  matrix products: 15.6 us -> 0 us
    pallas_call x0 -> x1, Pallas kernels: none -> 122 us  [on_device(): pl.pallas_call(functools.partial(kernel, dims), out_shape=(out_state, out...]
    ppermute x34 -> x0, starting transfers between devices: 87.7 us -> none  [the longest x16 63.3 us: padded(): before = lax.ppermute(last, axis, up)]
    reduce_sum x72 -> x0, other arithmetic: 66.7 us -> none  [the longest x16 25 us: contact(): jnp.sum(separation * separation, axis=0)]
    another operation x2 -> x0, loops' own time: 34.8 us -> none  [the longest x1 17.9 us: on_device(): lax.scan(backward_step, start_carry, (numbers, extended_all, velocity_all...]
    dynamic_slice x41 -> x0, local copies, waits for them, and re-layouts: 27.4 us -> none  [the longest x16 9.42 us: on_device(): lax.scan(forward_step, own_start, numbers)]
    psum x1 -> x0, blocking collectives: 18.2 us -> none  [on_device(): summed_row, summed_column = lax.psum((grad_row, column_own), 'section')]
    dot_general x64 -> x0, matrix products: 15.6 us -> none  [the longest x24 5.87 us: contact(): jnp.einsum('pt,ctk->cpk', hits_b, tiles_all, precision=lax.Precision.HIGH...]
    all_gather x2 -> x0, blocking collectives: 15.3 us -> none  [the longest x1 8.05 us: on_device(): lax.all_gather(contact_a, 'section', axis=0, tiled=True)]
  transfers between devices with their start and end apart: 36 -> 0, of which waited for: 10 -> 0; matrix products, arithmetic and copies ran while one was open for 7% -> 0% of each run, Pallas kernels for 0% -> 0%
where the time goes in v1:
time: 129 us
  Pallas kernels  122 us (95%)
  local copies, waits for them, and re-layouts  5.56 us (4%)
    pallas_call x1, Pallas kernels, on_device(): pl.pallas_call(functools.partial(kernel, dims), out_shape=(out_state, out...  122 us
    unnamed x14, local copies, waits for them, and re-layouts  4.96 us

profile of v1, /device:TPU:0, one launch (start us, length us, event | category | flops | bytes accessed | tf_op | source)
XLA Modules:
  0.0 128.6 jit_solution(18095545411708269895)
XLA Ops:
  0.6 0.0 copy-start.4
  0.6 0.0 copy-start.3
  0.7 0.6 copy-done.4
  1.3 0.0 copy-start.2
  1.3 0.1 copy.9
  1.4 0.0 copy-done.3
  1.4 0.6 copy-done.2
  2.0 0.1 pad_add_fusion
  2.0 0.6 pad.4.lists_ref
  2.6 122.3 %shard_map.85 = (f32[1,8,6,8,512]{4,3,2,1,0:T(8,128)}, f32[1,8,6,8,512]{4,3,2,1,0:T(8,128)}, f32[2,8,512]{2,1,0:T(8,128)}) custom-call(f32[8,6,8,512]{3,2,1,0:T(8,128)} %start_hbm.1, f32[2,8,512]{2,1,0:T(8,128)} %stiff_ref.1, s32[8,128]{1,0:T(8,128)} %pad.4.lists_ref, f32[8,6,8,512]{3,2,1,0:T(8,128)} %cot_hbm.1), custom_call_target="tpu_custom_call" | custom-call | tf_op jit(solution)/shard_map/pallas_call | solution.py:577
  124.9 0.0 copy-start
  125.0 2.1 %copy.13 = f32[1,8,6,8,512]{4,3,2,1,0:T(8,128)} copy(f32[1,8,6,8,512]{4,3,2,1,0:T(8,128)} %get-tuple-element.6) | data formatting | bytes 1572864
  127.1 0.0 copy-done
  127.1 0.0 copy-start.1
  127.1 0.9 copy.14
  128.0 0.0 copy-done.1
  128.0 0.6 copy.15
Async XLA Ops:
  0.6 0.7 copy-start.4
  0.6 0.7 copy-start.3
  1.3 0.7 copy-start.2
  124.9 2.1 %copy-start = (f32[1,8,6,8,512]{4,3,2,1,0:T(8,128)S(1)}, f32[1,8,6,8,512]{4,3,2,1,0:T(8,128)}, u32[]{:S(2)}) copy-start(f32[1,8,6,8,512]{4,3,2,1,0:T(8,128)} %get-tuple-element.7) | copy-start | bytes 2359300
  127.1 0.9 copy-start.1

commit v2 on v1

--- a/solution.py
+++ b/solution.py
@@ -1,4 +1,5 @@
 import functools
+import math
 
 import jax
 import jax.numpy as jnp
@@ -14,7 +15,7 @@
 gravity = 0.5
 tiny_length = 1e-06
 LANES = 128
-CHUNK = 32
+DEPTH = 8
 MESH = pl.DeviceIdType.MESH
 
 
@@ -37,12 +38,11 @@
     lists_all,
     lists_s,
     ext,
+    halo_in,
     vel,
     adj,
     exit_buf,
     adj_buf,
-    halo_out,
-    halo_in,
     back_out,
     back_in,
     above_out,
@@ -50,7 +50,6 @@
     upper_out,
     upper_in,
     grad_parts,
-    gath,
     force_adj,
     load_sem,
     smem_sem,
@@ -104,14 +103,27 @@
     def peer(k):
         return lax.rem(sec + k, sections)
 
-    def store_rows(ref, index, row, value):
+    def store_rows(ref, index, lead, part, value):
         for q in range(quarter):
-            part = value[:, q * LANES : (q + 1) * LANES]
-            ref[index + (q, slice(row, row + value.shape[0]), slice(None))] = part
-
-    def load_rows(ref, index, row, count):
-        parts = [ref[index + (q, slice(row, row + count), slice(None))] for q in range(quarter)]
+            ref[index + (pl.ds((lead + q) * DEPTH + part, rows, stride=quarter * DEPTH), slice(None))] = (
+                value[:, q * LANES : (q + 1) * LANES]
+            )
+
+    def load_rows(ref, index, lead, part, count):
+        parts = []
+        for q in range(quarter):
+            at = (lead + q) * DEPTH + part
+            where = pl.ds(at, 1) if count == 1 else pl.ds(at, count, stride=quarter * DEPTH)
+            parts.append(ref[index + (where, slice(None))])
         return jnp.concatenate(parts, axis=1)
+
+    def store_points(g, t, x):
+        for c in range(3):
+            store_rows(ext, (g, t), quarter, c, x[c])
+        store_rows(ext, (g, t), quarter, 3, square(x))
+
+    def square(d):
+        return d[0] * d[0] + d[1] * d[1] + d[2] * d[2]
 
     loads = []
     for t in range(share):
@@ -137,9 +149,9 @@
     above_out[...] = stiff_ref[1, rows - 1 : rows, :]
     above_in[...] = jnp.zeros_like(above_in)
     upper_in[...] = jnp.zeros_like(upper_in)
+    band = quarter * DEPTH
     halo_in[...] = jnp.zeros_like(halo_in)
     back_in[...] = jnp.zeros_like(back_in)
-    gath[...] = jnp.zeros_like(gath)
     lists_all[sec] = lists_ref[...]
     barrier = pltpu.get_barrier_semaphore()
     for k in range(1, sections):
@@ -156,26 +168,25 @@
     for copy in loads:
         copy.wait()
     for t in range(share):
-        for c in range(3):
-            now = exit_buf[0, t, c]
-            store_rows(ext, (0, t, c), 0, now)
-            halo_out[0, t, 0, c : c + 1, :] = now[0:1]
-            halo_out[0, t, 1, c : c + 1, :] = now[rows - 1 : rows]
+        store_points(0, t, [exit_buf[0, t, c] for c in range(3)])
 
     greeted = jnp.where(has_up, 1, 0) + jnp.where(has_down, 1, 0)
     pl.semaphore_wait(barrier, sections - 1 + greeted)
 
+    def part_of(ref, g, t, side):
+        if ref is not ext:
+            return ref.at[g, t, side]
+        return ref.at[g, t, pl.ds(band * (1 if side == 0 else rows), band)]
+
     def to_up(out, into, send, recv, g, t):
-        return remote(
-            out.at[g, t, 0], into.at[g, t, 1], send.at[g, t, 0], recv.at[g, t, 1], (sec, spc - 1)
-        )
+        source, target = part_of(out, g, t, 0), part_of(into, g, t, 1)
+        return remote(source, target, send.at[g, t, 0], recv.at[g, t, 1], (sec, spc - 1))
 
     def to_down(out, into, send, recv, g, t):
-        return remote(
-            out.at[g, t, 1], into.at[g, t, 0], send.at[g, t, 1], recv.at[g, t, 0], (sec, spc + 1)
-        )
-
-    halo = (halo_out, halo_in, halo_send, halo_recv)
+        source, target = part_of(out, g, t, 1), part_of(into, g, t, 0)
+        return remote(source, target, send.at[g, t, 1], recv.at[g, t, 0], (sec, spc + 1))
+
+    halo = (ext, halo_in, halo_send, halo_recv)
     back = (back_out, back_in, back_send, back_recv)
 
     def exchange(kind, g, t):
@@ -192,15 +203,13 @@
 
         @pl.when(has_up)
         def _():
-            remote(
-                out.at[g, t, 1], into.at[g, t, 0], send.at[g, t, 1], recv.at[g, t, 0], (sec, spc - 1)
-            ).wait_recv()
+            source, target = part_of(out, g, t, 1), part_of(into, g, t, 0)
+            remote(source, target, send.at[g, t, 1], recv.at[g, t, 0], (sec, spc - 1)).wait_recv()
 
         @pl.when(has_down)
         def _():
-            remote(
-                out.at[g, t, 0], into.at[g, t, 1], send.at[g, t, 0], recv.at[g, t, 1], (sec, spc + 1)
-            ).wait_recv()
+            source, target = part_of(out, g, t, 0), part_of(into, g, t, 1)
+            remote(source, target, send.at[g, t, 0], recv.at[g, t, 1], (sec, spc + 1)).wait_recv()
 
     def sent(kind, g, t):
         @pl.when(has_up)
@@ -264,9 +273,6 @@
     def above(value):
         return pltpu.roll(value, 1, 0)
 
-    def square(d):
-        return d[0] * d[0] + d[1] * d[1] + d[2] * d[2]
-
     def contact_slot(g, t, p):
         ordinal = g // steps_section
         inner = lax.rem(g, steps_section)
@@ -275,24 +281,62 @@
         live = jnp.where(p < lists_s[ordinal, inner, 2 * pairs], 1.0, 0.0)
         return first, second, live
 
-    def tile_rows(ref, index, row, column):
-        return [
-            ref[index + (c, column, pl.ds(row, 1), slice(None))]
-            for c in range(3)
-        ]
-
-    def gather_others(g, t):
-        for p in range(pairs):
-            _, second, _ = contact_slot(g, t, p)
-            row = second // quarter
-            column = lax.rem(second, quarter)
-            place = jnp.where(
-                row == 0, rows, jnp.where(row == rows + 1, rows + 1, row - 1)
-            )
-            found = tile_rows(ext, (g, t), place, column)
-            for c in range(3):
-                gath[4 * p + c : 4 * p + c + 1, :] = found[c]
-        return gath[...].T
+    part_id = lax.broadcasted_iota(jnp.int32, (DEPTH, LANES), 0)
+
+    def block(ref, index, tile):
+        at = tile * DEPTH
+        return ref[index + (pl.ds(at, DEPTH), slice(None))]
+
+    def point_block(g, t, tile):
+        found = block(ext, (g, t), tile)
+        return jnp.where(part_id < 4, found, jnp.where(part_id == 4, 1.0, 0.0))
+
+    def pieces(value):
+        one = value.astype(jnp.bfloat16).astype(jnp.float32)
+        rest = value - one
+        two = rest.astype(jnp.bfloat16).astype(jnp.float32)
+        return one, two, rest - two
+
+    def left_stack(u):
+        return jnp.concatenate([u[0], u[0], u[1], u[1], u[0], u[2]], axis=0).astype(jnp.bfloat16)
+
+    def right_stack(v):
+        return jnp.concatenate([v[0], v[1], v[0], v[1], v[2], v[0]], axis=0).astype(jnp.bfloat16)
+
+    def sum_stack(u):
+        whole = jnp.concatenate([u[0], u[1], u[2], jnp.zeros_like(u[0])], axis=0)
+        whole = whole.astype(jnp.bfloat16)
+        return jnp.concatenate([whole, whole], axis=1)
+
+    def halves(value):
+        one = value.astype(jnp.bfloat16)
+        return one, (value - one.astype(jnp.float32)).astype(jnp.bfloat16)
+
+    def multiply(left, right, over_left, over_right):
+        return lax.dot_general(
+            left,
+            right,
+            (((over_left,), (over_right,)), ((), ())),
+            preferred_element_type=jnp.float32,
+        )
+
+    def folded(value):
+        return value[0:DEPTH] + value[DEPTH : 2 * DEPTH] + value[2 * DEPTH : 3 * DEPTH]
+
+    def over_others(stack, parts):
+        return folded(multiply(stack, jnp.concatenate(parts, axis=0), 1, 0))
+
+    def over_own(stack, parts):
+        return folded(multiply(stack, jnp.concatenate(parts, axis=1), 1, 1))
+
+    power = -1.0 / (kernel_spread * math.log(2.0))
+
+    def distance_block(own):
+        return jnp.where(
+            part_id < 3,
+            own * (-2.0 * power),
+            jnp.where(part_id == 3, power, jnp.where(part_id == 4, own[3:4] * power, 0.0)),
+        )
 
     def wide(value):
         return jnp.concatenate([value] * quarter, axis=1)
@@ -301,12 +345,11 @@
 
     def forward_one(g, t):
         arrive(halo, g, t)
-        for side in range(2):
-            for c in range(3):
-                store_rows(ext, (g, t, c), rows + side, halo_in[g, t, side, c : c + 1, :])
-        x = [load_rows(ext, (g, t, c), 0, rows) for c in range(3)]
-        up = [load_rows(ext, (g, t, c), rows, 1) for c in range(3)]
-        down = [load_rows(ext, (g, t, c), rows + 1, 1) for c in range(3)]
+        ext[g, t, 0:band, :] = halo_in[g, t, 0]
+        ext[g, t, (rows + 1) * band : (rows + 2) * band, :] = halo_in[g, t, 1]
+        x = [load_rows(ext, (g, t), quarter, c, rows) for c in range(3)]
+        up = [load_rows(ext, (g, t), 0, c, 1) for c in range(3)]
+        down = [load_rows(ext, (g, t), (rows + 1) * quarter, c, 1) for c in range(3)]
         k_row = stiff_ref[0] * column_mask
         k_column = stiff_ref[1] * row_mask
         d = [right_of(v) - v for v in x]
@@ -322,32 +365,30 @@
             force[c] + pulls[c] + jnp.where(first_row, pull * d[c], -above(pulls[c]))
             for c in range(3)
         ]
-        columns = gather_others(g, t)
         for p in range(pairs):
-            first, _, live = contact_slot(g, t, p)
-            own = tile_rows(ext, (g, t), first // quarter, lax.rem(first, quarter))
-            sums = None
-            for j in range(0, LANES, CHUNK):
-                s = [own[c] - columns[j : j + CHUNK, 4 * p + c : 4 * p + c + 1] for c in range(3)]
-                weight = jnp.exp(square(s) * (-1.0 / kernel_spread))
-                terms = [weight * v for v in s]
-                sums = terms if sums is None else [a + b for a, b in zip(sums, terms)]
+            first, second, live = contact_slot(g, t, p)
+            own = point_block(g, t, first + quarter)
+            other = pieces(point_block(g, t, second))
+            weight = jnp.exp2(
+                multiply(left_stack(other), right_stack(pieces(distance_block(own))), 0, 0)
+            )
+            sums = over_others(sum_stack(other), halves(weight))
+            repulsion = (coefficient * live) * (own * sums[4:5] - sums)
             here = tile_id == first
             for c in range(3):
-                repulsion = (coefficient * live) * jnp.sum(sums[c], axis=0, keepdims=True)
-                force[c] = force[c] + jnp.where(here, wide(repulsion), 0.0)
+                force[c] = force[c] + jnp.where(here, wide(repulsion[c : c + 1]), 0.0)
         force[2] = force[2] - gravity
         ordinal = g // steps_section
         leaving = lax.rem(g, steps_section) == steps_section - 1
+        points = []
         for c in range(3):
             moved = damping * (vel[t, c] + time_step * force[c])
             point = x[c] + time_step * moved
             vel[t, c] = moved
-            store_rows(ext, (g + 1, t, c), 0, point)
-            halo_out[g + 1, t, 0, c : c + 1, :] = point[0:1]
-            halo_out[g + 1, t, 1, c : c + 1, :] = point[rows - 1 : rows]
+            points.append(point)
             exit_buf[ordinal, t, c] = point
             exit_buf[ordinal, t, 3 + c] = moved
+        store_points(g + 1, t, points)
 
         @pl.when(g < steps - 1)
         def _():
@@ -425,15 +466,15 @@
             adj_buf[ordinal, t, 3 + c] = passed
             f.append(time_step * passed)
         for c in range(3):
-            store_rows(force_adj, (t, c), 0, f[c])
+            store_rows(force_adj, (t,), 0, c, f[c])
 
         @pl.when(lax.rem(g, steps_section) == 0)
         def _():
             deliver(adj_buf, adj_hbm, adj_send, adj_recv, 1, ordinal, t, 3, 3)
 
-        x = [load_rows(ext, (g, t, c), 0, rows) for c in range(3)]
-        up = [load_rows(ext, (g, t, c), rows, 1) for c in range(3)]
-        down = [load_rows(ext, (g, t, c), rows + 1, 1) for c in range(3)]
+        x = [load_rows(ext, (g, t), quarter, c, rows) for c in range(3)]
+        up = [load_rows(ext, (g, t), 0, c, 1) for c in range(3)]
+        down = [load_rows(ext, (g, t), (rows + 1) * quarter, c, 1) for c in range(3)]
 
         def edge(d, phi, constant):
             inverse = lax.rsqrt(square(d) + tiny_length)
@@ -458,32 +499,40 @@
             out[c] - offset[c] + jnp.where(first_row, -up_adj[c], above(offset[c]))
             for c in range(3)
         ]
-        columns = gather_others(g, t)
         ghost = [jnp.zeros((rows, width), jnp.float32) for _ in range(3)]
         for p in range(pairs):
             first, second, live = contact_slot(g, t, p)
-            row, column = first // quarter, lax.rem(first, quarter)
-            own = tile_rows(ext, (g, t), row, column)
-            scale = coefficient * live
-            pulled = [scale * v for v in tile_rows(force_adj, (t,), row, column)]
-            sums = None
-            across = []
-            for j in range(0, LANES, CHUNK):
-                s = [own[c] - columns[j : j + CHUNK, 4 * p + c : 4 * p + c + 1] for c in range(3)]
-                weight = jnp.exp(square(s) * (-1.0 / kernel_spread))
-                along = s[0] * pulled[0] + s[1] * pulled[1] + s[2] * pulled[2]
-                terms = [weight * (pulled[c] - along * s[c]) for c in range(3)]
-                sums = terms if sums is None else [a + b for a, b in zip(sums, terms)]
-                across.append([jnp.sum(v, axis=1, keepdims=True) for v in terms])
+            own = point_block(g, t, first + quarter)
+            other_block = point_block(g, t, second)
+            other = pieces(other_block)
+            pulled = jnp.where(part_id < 3, (coefficient * live) * block(force_adj, (t,), first), 0.0)
+            along = jnp.sum(own * pulled, axis=0, keepdims=True)
+            along = jnp.where(part_id == 4, along, -pulled)
+            right = jnp.concatenate(
+                [right_stack(pieces(distance_block(own))), right_stack(pieces(along))], axis=1
+            )
+            both = multiply(left_stack(other), right, 0, 0)
+            weight = jnp.exp2(both[:, :LANES])
+            moment = weight * both[:, LANES:]
+            weight_parts, moment_parts = halves(weight), halves(moment)
+            stack = sum_stack(other)
+            weight_sum = over_others(stack, weight_parts)
+            moment_sum = over_others(stack, moment_parts)
+            gain = pulled * weight_sum[4:5] - own * moment_sum[4:5] + moment_sum
+            weight_sum = over_own(sum_stack(pieces(pulled)), weight_parts)
+            moment_sum = over_own(sum_stack(pieces(own)), moment_parts)
+            loss = weight_sum - moment_sum + other_block * moment_sum[4:5]
             here = tile_id == first
             there = tile_id == second - quarter
             outside = halo_tile == second
             for c in range(3):
-                gain = wide(jnp.sum(sums[c], axis=0, keepdims=True))
-                loss = jnp.concatenate([a[c] for a in across], axis=0)
-                loss = wide(jnp.broadcast_to(loss, (LANES, 8)).T[0:1])
-                out[c] = out[c] + jnp.where(here, gain, 0.0) - jnp.where(there, loss, 0.0)
-                ghost[c] = ghost[c] - jnp.where(outside, loss, 0.0)
+                lost = wide(loss[c : c + 1])
+                out[c] = (
+                    out[c]
+                    + jnp.where(here, wide(gain[c : c + 1]), 0.0)
+                    - jnp.where(there, lost, 0.0)
+                )
+                ghost[c] = ghost[c] - jnp.where(outside, lost, 0.0)
         for c in range(3):
             adj[t, c] = out[c]
             back_out[g, t, 0, c : c + 1, :] = up_adj[c] + ghost[c][0:1]
@@ -582,13 +631,12 @@
         scratch_shapes=[
             pltpu.VMEM((sections, 8, LANES), jnp.int32),
             pltpu.SMEM((sections, 8, LANES), jnp.int32),
-            pltpu.VMEM((steps + 1, share, 3, width // LANES, 2 * rows, LANES), f32),
+            pltpu.VMEM((steps + 1, share, (rows + 2) * width // LANES * DEPTH, LANES), f32),
+            pltpu.VMEM((steps, share, 2, width // LANES * DEPTH, LANES), f32),
             pltpu.VMEM((share, 3, rows, width), f32),
             pltpu.VMEM((share, parts, rows, width), f32),
             pltpu.VMEM((sections, share, parts, rows, width), f32),
             pltpu.VMEM((sections, share, parts, rows, width), f32),
-            pltpu.VMEM((steps + 1, share, 2, 3, width), f32),
-            pltpu.VMEM((steps, share, 2, 3, width), f32),
             pltpu.VMEM((steps, share, 2, 3, width), f32),
             pltpu.VMEM((steps, share, 2, 3, width), f32),
             pltpu.VMEM((1, width), f32),
@@ -596,8 +644,7 @@
             pltpu.VMEM((1, width), f32),
             pltpu.VMEM((1, width), f32),
             pltpu.VMEM((sections, 2, rows, width), f32),
-            pltpu.VMEM((LANES, LANES), f32),
-            pltpu.VMEM((share, 3, width // LANES, rows, LANES), f32),
+            pltpu.VMEM((share, rows * width // LANES * DEPTH, LANES), f32),
             dma((2, share, 3)),
             dma,
             dma((sections - 1,)),

time: 129 us -> 80 us (0.62)
  Pallas kernels: 122 us -> 73.2 us
    pallas_call x1, Pallas kernels: 122 us -> 73.2 us  [on_device(): pl.pallas_call(functools.partial(kernel, dims), out_shape=(out_state, out...]
where the time goes in v2:
time: 80 us; the launch traced here: 79.5 us
  Pallas kernels  73.2 us (92%)
  local copies, waits for them, and re-layouts  5.56 us (7%)
    pallas_call x1, Pallas kernels, on_device(): pl.pallas_call(functools.partial(kernel, dims), out_shape=(out_state, out...  73.2 us
    unnamed x14, local copies, waits for them, and re-layouts  4.96 us

profile of v2, /device:TPU:0, one launch (start us, length us, event | category | flops | bytes accessed | tf_op | source)
XLA Modules:
  0.0 79.5 jit_solution(6326922574341508723)
XLA Ops:
  0.6 0.0 copy-start.4
  0.6 0.0 copy-start.3
  0.7 0.6 copy-done.4
  1.3 0.0 copy-start.2
  1.3 0.1 copy.9
  1.4 0.0 copy-done.3
  1.4 0.6 copy-done.2
  2.0 0.1 pad_add_fusion
  2.0 0.6 pad.4.lists_ref
  2.6 73.2 %shard_map.85 = (f32[1,8,6,8,512]{4,3,2,1,0:T(8,128)}, f32[1,8,6,8,512]{4,3,2,1,0:T(8,128)}, f32[2,8,512]{2,1,0:T(8,128)}) custom-call(f32[8,6,8,512]{3,2,1,0:T(8,128)} %start_hbm.1, f32[2,8,512]{2,1,0:T(8,128)} %stiff_ref.1, s32[8,128]{1,0:T(8,128)} %pad.4.lists_ref, f32[8,6,8,512]{3,2,1,0:T(8,128)} %cot_hbm.1), custom_call_target="tpu_custom_call" | custom-call | tf_op jit(solution)/shard_map/pallas_call | solution.py:626
  75.9 0.0 copy-start
  75.9 2.1 %copy.13 = f32[1,8,6,8,512]{4,3,2,1,0:T(8,128)} copy(f32[1,8,6,8,512]{4,3,2,1,0:T(8,128)} %get-tuple-element.6) | data formatting | bytes 1572864
  78.0 0.0 copy-done
  78.0 0.0 copy-start.1
  78.0 0.9 %copy.14 = f32[1,8,6,8,512]{4,3,2,1,0:T(8,128)} copy(f32[1,8,6,8,512]{4,3,2,1,0:T(8,128)S(1)} %copy-done) | data formatting | bytes 1572864
  78.9 0.0 copy-done.1
  78.9 0.6 copy.15
Async XLA Ops:
  0.6 0.7 copy-start.4
  0.6 0.7 copy-start.3
  1.3 0.7 copy-start.2
  75.9 2.1 %copy-start = (f32[1,8,6,8,512]{4,3,2,1,0:T(8,128)S(1)}, f32[1,8,6,8,512]{4,3,2,1,0:T(8,128)}, u32[]{:S(2)}) copy-start(f32[1,8,6,8,512]{4,3,2,1,0:T(8,128)} %get-tuple-element.7) | copy-start | bytes 2359300
  78.0 0.9 %copy-start.1 = (f32[2,8,512]{2,1,0:T(8,128)S(1)}, f32[2,8,512]{2,1,0:T(8,128)}, u32[]{:S(2)}) copy-start(f32[2,8,512]{2,1,0:T(8,128)} %get-tuple-element.8) | copy-start | bytes 98308

commit v3 on v2

--- a/solution.py
+++ b/solution.py
@@ -51,6 +51,7 @@
     upper_in,
     grad_parts,
     force_adj,
+    scat,
     load_sem,
     smem_sem,
     list_send,
@@ -84,12 +85,6 @@
     tile_id = row_id * quarter + tile_in_row
     first_row = row_id == 0
     last_row = row_id == rows - 1
-    halo_tile = jnp.where(
-        first_row,
-        tile_in_row,
-        jnp.where(row_id == 1, tile_in_row + (rows + 1) * quarter, -1),
-    )
-
     def remote(src, dst, send, recv, device):
         return pltpu.make_async_remote_copy(
             src_ref=src,
@@ -338,8 +333,35 @@
             jnp.where(part_id == 3, power, jnp.where(part_id == 4, own[3:4] * power, 0.0)),
         )
 
-    def wide(value):
-        return jnp.concatenate([value] * quarter, axis=1)
+    tiles_all = (rows + 2) * quarter
+
+    def place(blocks, tiles):
+        depth = len(blocks) * DEPTH
+        lane = lax.broadcasted_iota(jnp.int32, (1, depth), 1)
+        slot = lax.shift_right_logical(lane, DEPTH.bit_length() - 1)
+        part = jnp.bitwise_and(lane, DEPTH - 1)
+        code = jnp.zeros_like(lane)
+        for number, tile in enumerate(tiles):
+            code = jnp.where(slot == number, tile, code)
+        code = jnp.where(part < 3, code + part * tiles_all, -1)
+        target = lax.broadcasted_iota(jnp.int32, (3 * tiles_all, depth), 0)
+        hits = jnp.where(target == code, 1.0, 0.0)
+        hits = jnp.concatenate([hits, hits], axis=1).astype(jnp.bfloat16)
+        values = jnp.concatenate(halves(jnp.concatenate(blocks, axis=0)), axis=0)
+        scat[...] = multiply(hits, values, 1, 0)
+
+    def placed(c):
+        return jnp.concatenate(
+            [
+                scat[pl.ds(c * tiles_all + quarter + q, rows, stride=quarter), :]
+                for q in range(quarter)
+            ],
+            axis=1,
+        )
+
+    def placed_row(c, row):
+        at = c * tiles_all + row * quarter
+        return jnp.concatenate([scat[at + q : at + q + 1, :] for q in range(quarter)], axis=1)
 
     coefficient = 2.0 * contact_scale / kernel_spread
 
@@ -347,6 +369,18 @@
         arrive(halo, g, t)
         ext[g, t, 0:band, :] = halo_in[g, t, 0]
         ext[g, t, (rows + 1) * band : (rows + 2) * band, :] = halo_in[g, t, 1]
+        given, taken = [], []
+        for p in range(pairs):
+            first, second, live = contact_slot(g, t, p)
+            own = point_block(g, t, first + quarter)
+            other = pieces(point_block(g, t, second))
+            weight = jnp.exp2(
+                multiply(left_stack(other), right_stack(pieces(distance_block(own))), 0, 0)
+            )
+            sums = over_others(sum_stack(other), halves(weight))
+            given.append((coefficient * live) * (own * sums[4:5] - sums))
+            taken.append(first + quarter)
+        place(given, taken)
         x = [load_rows(ext, (g, t), quarter, c, rows) for c in range(3)]
         up = [load_rows(ext, (g, t), 0, c, 1) for c in range(3)]
         down = [load_rows(ext, (g, t), (rows + 1) * quarter, c, 1) for c in range(3)]
@@ -362,21 +396,9 @@
         d = [up[c] - x[c][0:1] for c in range(3)]
         pull = above_in[...] * (1.0 - lax.rsqrt(square(d) + tiny_length))
         force = [
-            force[c] + pulls[c] + jnp.where(first_row, pull * d[c], -above(pulls[c]))
+            force[c] + pulls[c] + jnp.where(first_row, pull * d[c], -above(pulls[c])) + placed(c)
             for c in range(3)
         ]
-        for p in range(pairs):
-            first, second, live = contact_slot(g, t, p)
-            own = point_block(g, t, first + quarter)
-            other = pieces(point_block(g, t, second))
-            weight = jnp.exp2(
-                multiply(left_stack(other), right_stack(pieces(distance_block(own))), 0, 0)
-            )
-            sums = over_others(sum_stack(other), halves(weight))
-            repulsion = (coefficient * live) * (own * sums[4:5] - sums)
-            here = tile_id == first
-            for c in range(3):
-                force[c] = force[c] + jnp.where(here, wide(repulsion[c : c + 1]), 0.0)
         force[2] = force[2] - gravity
         ordinal = g // steps_section
         leaving = lax.rem(g, steps_section) == steps_section - 1
@@ -472,34 +494,7 @@
         def _():
             deliver(adj_buf, adj_hbm, adj_send, adj_recv, 1, ordinal, t, 3, 3)
 
-        x = [load_rows(ext, (g, t), quarter, c, rows) for c in range(3)]
-        up = [load_rows(ext, (g, t), 0, c, 1) for c in range(3)]
-        down = [load_rows(ext, (g, t), (rows + 1) * quarter, c, 1) for c in range(3)]
-
-        def edge(d, phi, constant):
-            inverse = lax.rsqrt(square(d) + tiny_length)
-            bend = 1.0 - inverse
-            along = d[0] * phi[0] + d[1] * phi[1] + d[2] * phi[2]
-            twist = inverse * inverse * inverse * along
-            return bend * along, [constant * (bend * phi[c] + twist * d[c]) for c in range(3)]
-
-        d = [right_of(v) - v for v in x]
-        part, offset = edge(d, [v - right_of(v) for v in f], stiff_ref[0] * column_mask)
-        grad_row = grad_row + part
-        out = [point_adj[c] - offset[c] + left_of(offset[c]) for c in range(3)]
-        d = [jnp.where(last_row, down[c], below(x[c])) - x[c] for c in range(3)]
-        phi = [v - jnp.where(last_row, 0.0, below(v)) for v in f]
-        part, offset = edge(d, phi, stiff_ref[1] * row_mask)
-        grad_column = grad_column + part
-        down_adj = [offset[c][rows - 1 : rows] for c in range(3)]
-        d = [up[c] - x[c][0:1] for c in range(3)]
-        part, up_adj = edge(d, [v[0:1] for v in f], above_in[...])
-        grad_upper = grad_upper + part
-        out = [
-            out[c] - offset[c] + jnp.where(first_row, -up_adj[c], above(offset[c]))
-            for c in range(3)
-        ]
-        ghost = [jnp.zeros((rows, width), jnp.float32) for _ in range(3)]
+        gains, losses, receivers, sources = [], [], [], []
         for p in range(pairs):
             first, second, live = contact_slot(g, t, p)
             own = point_block(g, t, first + quarter)
@@ -515,28 +510,51 @@
             weight = jnp.exp2(both[:, :LANES])
             moment = weight * both[:, LANES:]
             weight_parts, moment_parts = halves(weight), halves(moment)
-            stack = sum_stack(other)
-            weight_sum = over_others(stack, weight_parts)
-            moment_sum = over_others(stack, moment_parts)
-            gain = pulled * weight_sum[4:5] - own * moment_sum[4:5] + moment_sum
-            weight_sum = over_own(sum_stack(pieces(pulled)), weight_parts)
-            moment_sum = over_own(sum_stack(pieces(own)), moment_parts)
-            loss = weight_sum - moment_sum + other_block * moment_sum[4:5]
-            here = tile_id == first
-            there = tile_id == second - quarter
-            outside = halo_tile == second
-            for c in range(3):
-                lost = wide(loss[c : c + 1])
-                out[c] = (
-                    out[c]
-                    + jnp.where(here, wide(gain[c : c + 1]), 0.0)
-                    - jnp.where(there, lost, 0.0)
-                )
-                ghost[c] = ghost[c] - jnp.where(outside, lost, 0.0)
+            pair_parts = [
+                jnp.concatenate([a, b], axis=1) for a, b in zip(weight_parts, moment_parts)
+            ]
+            sums = over_others(sum_stack(other), pair_parts)
+            weight_sum, moment_sum = sums[:, :LANES], sums[:, LANES:]
+            gains.append(pulled * weight_sum[4:5] - own * moment_sum[4:5] + moment_sum)
+            stack = jnp.concatenate(
+                [sum_stack(pieces(pulled)), sum_stack(pieces(-own))], axis=1
+            )
+            back_sums = over_own(stack, weight_parts + moment_parts)
+            losses.append(other_block * back_sums[4:5] - back_sums)
+            receivers.append(first + quarter)
+            sources.append(second)
+        place(gains + losses, receivers + sources)
+        x = [load_rows(ext, (g, t), quarter, c, rows) for c in range(3)]
+        up = [load_rows(ext, (g, t), 0, c, 1) for c in range(3)]
+        down = [load_rows(ext, (g, t), (rows + 1) * quarter, c, 1) for c in range(3)]
+
+        def edge(d, phi, constant):
+            inverse = lax.rsqrt(square(d) + tiny_length)
+            bend = 1.0 - inverse
+            along = d[0] * phi[0] + d[1] * phi[1] + d[2] * phi[2]
+            twist = inverse * inverse * inverse * along
+            return bend * along, [constant * (bend * phi[c] + twist * d[c]) for c in range(3)]
+
+        d = [right_of(v) - v for v in x]
+        part, offset = edge(d, [v - right_of(v) for v in f], stiff_ref[0] * column_mask)
+        grad_row = grad_row + part
+        out = [point_adj[c] - offset[c] + left_of(offset[c]) for c in range(3)]
+        d = [jnp.where(last_row, down[c], below(x[c])) - x[c] for c in range(3)]
+        phi = [v - jnp.where(last_row, 0.0, below(v)) for v in f]
+        part, offset = edge(d, phi, stiff_ref[1] * row_mask)
+        grad_column = grad_column + part
+        down_adj = [offset[c][rows - 1 : rows] for c in range(3)]
+        d = [up[c] - x[c][0:1] for c in range(3)]
+        part, up_adj = edge(d, [v[0:1] for v in f], above_in[...])
+        grad_upper = grad_upper + part
+        out = [
+            out[c] - offset[c] + jnp.where(first_row, -up_adj[c], above(offset[c])) + placed(c)
+            for c in range(3)
+        ]
         for c in range(3):
             adj[t, c] = out[c]
-            back_out[g, t, 0, c : c + 1, :] = up_adj[c] + ghost[c][0:1]
-            back_out[g, t, 1, c : c + 1, :] = down_adj[c] + ghost[c][1:2]
+            back_out[g, t, 0, c : c + 1, :] = up_adj[c] + placed_row(c, 0)
+            back_out[g, t, 1, c : c + 1, :] = down_adj[c] + placed_row(c, rows + 1)
         exchange(back, g, t)
         return grad_row, grad_column, grad_upper
 
@@ -645,6 +663,7 @@
             pltpu.VMEM((1, width), f32),
             pltpu.VMEM((sections, 2, rows, width), f32),
             pltpu.VMEM((share, rows * width // LANES * DEPTH, LANES), f32),
+            pltpu.VMEM((3 * (rows + 2) * width // LANES, LANES), f32),
             dma((2, share, 3)),
             dma,
             dma((sections - 1,)),

time: 80 us -> 79.7 us (level)
  no operation moved by 1% of the time
where the time goes in v3:
time: 79.7 us; the launch traced here: 79.3 us
  Pallas kernels  73 us (92%)
  local copies, waits for them, and re-layouts  5.56 us (7%)
    pallas_call x1, Pallas kernels, on_device(): pl.pallas_call(functools.partial(kernel, dims), out_shape=(out_state, out...  73 us
    unnamed x14, local copies, waits for them, and re-layouts  4.96 us

profile of v3, /device:TPU:0, one launch (start us, length us, event | category | flops | bytes accessed | tf_op | source)
XLA Modules:
  0.0 79.3 jit_solution(3288579166001817528)
XLA Ops:
  0.6 0.0 copy-start.4
  0.6 0.0 copy-start.3
  0.7 0.6 copy-done.4
  1.3 0.0 copy-start.2
  1.3 0.1 copy.9
  1.4 0.0 copy-done.3
  1.4 0.6 copy-done.2
  2.0 0.1 pad_add_fusion
  2.0 0.6 pad.4.lists_ref
  2.6 73.0 %shard_map.85 = (f32[1,8,6,8,512]{4,3,2,1,0:T(8,128)}, f32[1,8,6,8,512]{4,3,2,1,0:T(8,128)}, f32[2,8,512]{2,1,0:T(8,128)}) custom-call(f32[8,6,8,512]{3,2,1,0:T(8,128)} %start_hbm.1, f32[2,8,512]{2,1,0:T(8,128)} %stiff_ref.1, s32[8,128]{1,0:T(8,128)} %pad.4.lists_ref, f32[8,6,8,512]{3,2,1,0:T(8,128)} %cot_hbm.1), custom_call_target="tpu_custom_call" | custom-call | tf_op jit(solution)/shard_map/pallas_call | solution.py:644
  75.7 0.0 copy-start
  75.7 2.1 %copy.13 = f32[1,8,6,8,512]{4,3,2,1,0:T(8,128)} copy(f32[1,8,6,8,512]{4,3,2,1,0:T(8,128)} %get-tuple-element.6) | data formatting | bytes 1572864
  77.8 0.0 copy-done
  77.8 0.0 copy-start.1
  77.8 0.9 %copy.14 = f32[1,8,6,8,512]{4,3,2,1,0:T(8,128)} copy(f32[1,8,6,8,512]{4,3,2,1,0:T(8,128)S(1)} %copy-done) | data formatting | bytes 1572864
  78.7 0.0 copy-done.1
  78.7 0.6 copy.15
Async XLA Ops:
  0.6 0.7 copy-start.4
  0.6 0.7 copy-start.3
  1.3 0.7 copy-start.2
  75.7 2.1 %copy-start = (f32[1,8,6,8,512]{4,3,2,1,0:T(8,128)S(1)}, f32[1,8,6,8,512]{4,3,2,1,0:T(8,128)}, u32[]{:S(2)}) copy-start(f32[1,8,6,8,512]{4,3,2,1,0:T(8,128)} %get-tuple-element.7) | copy-start | bytes 2359300
  77.8 0.9 %copy-start.1 = (f32[2,8,512]{2,1,0:T(8,128)S(1)}, f32[2,8,512]{2,1,0:T(8,128)}, u32[]{:S(2)}) copy-start(f32[2,8,512]{2,1,0:T(8,128)} %get-tuple-element.8) | copy-start | bytes 98308
